TPU v7x, 1024 devices: a whole 4x4x32 slice. The times are simulated.
1024 devices in a mesh: section: 16 (over y_lo, x, core), expert: 64 (over y_hi, z).
Axes of the slice: x: 4, y: 4 (y_hi: 2, y_lo: 2; y = y_hi * 2 + y_lo), z: 32, core: 2. Of those that a mesh axis runs over, the one named last changes fastest.
Arguments:
- tokens: bfloat16 [2, 16, 4096, 2048], P(None, 'section', 'expert'), may hold values from -24 to 24
- norm_gain: float32 [2048], replicated, may hold values from 0.1 to 1.9
- expert_ids: int32 [2, 16, 4096, 2], P(None, 'section', 'expert'), may hold values from 0 to 23, all different within a row; in each aligned block of 64 rows (0 to 63, 64 to 127, ..., all dimensions but the last counted through in order) at most 6 rows name the same one
- route_scores: float32 [2, 16, 4096, 2], P(None, 'section', 'expert'), may hold values from 0.1 to 1
- placement: int32 [64], replicated, may hold values from 0 to 23, as said below
- w_gate: bfloat16 [64, 2048, 768], P('expert'), as said below
- w_up: bfloat16 [64, 2048, 768], P('expert'), as said below
- w_down: bfloat16 [64, 768, 2048], P('expert'), as said below
Outputs:
- onward: bfloat16 [2, 16, 4096, 2048], P(None, 'section', 'expert')
Inputs may be any that keep to these rules, and one draw needn't show every extreme that they name: `expert_ids`: in each micro-batch and section, the 64 rows of one device name each expert at most 6 times, a bound that some block reaches. `placement`: every expert holds two or more slots. `w_gate`: slots with equal placement hold equal gate projections. `w_up`: slots with equal placement hold equal up projections. `w_down`: slots with equal placement hold equal down projections.
All inputs are finite; a program needn't handle non-finite values.
Results may differ from a plain program's by a relative error of at most 0.0039.
Values may be sent and summed in bfloat16 or wider, within the bound.
No kernel may reach another device: no remote copies, remote signals or barrier semaphores. Data moves between devices by JAX's collectives and lax.ppermute only.
A program may use at most 64 MiB of HBM per device.

v0:
```python
import jax
import jax.numpy as jnp
from jax import lax
from jax.sharding import PartitionSpec as P

EPSILON = 1e-06


def passed_along(x, axis, by):
    peers = lax.axis_size(axis)
    pairs = [(i, i + by) for i in range(peers) if 0 <= i + by < peers]
    return lax.ppermute(x, axis, pairs)


def normalize(rows, gain):
    values = rows.astype(jnp.float32)
    scale = lax.rsqrt(jnp.mean(values * values, axis=-1, keepdims=True) + EPSILON)
    return (values * scale * gain).astype(jnp.bfloat16)


def exclusive_rank(onehot):
    before = jnp.cumsum(onehot, axis=0) - onehot
    return jnp.sum(before * onehot, axis=1)


def route_rows(chosen, placement, experts, capacity):
    flat_ids = chosen.reshape(-1)
    slot_count = placement.shape[0]
    expert_range = jnp.arange(experts, dtype=jnp.int32)
    slot_range = jnp.arange(slot_count, dtype=jnp.int32)
    expert_hit = (flat_ids[:, None] == expert_range[None, :]).astype(jnp.int32)
    owner_hit = (placement[:, None] == expert_range[None, :]).astype(jnp.int32)
    replica_rank = exclusive_rank(owner_hit)
    copies = jnp.sum(owner_hit, axis=0)
    row_copies = jnp.sum(expert_hit * copies[None, :], axis=1)
    wanted = exclusive_rank(expert_hit) % row_copies
    matches = (placement[None, :] == flat_ids[:, None]) & (replica_rank[None, :] == wanted[:, None])
    target = jnp.sum(jnp.where(matches, slot_range[None, :], 0), axis=1)
    target_hit = (target[:, None] == slot_range[None, :]).astype(jnp.int32)
    position = exclusive_rank(target_hit)
    return (target * capacity + position).reshape(chosen.shape)


def body(tokens, norm_gain, expert_ids, route_scores, placement, w_gate, w_up, w_down):
    devices = lax.axis_size("expert")
    slot_dev = w_gate.shape[0]
    slot_count = placement.shape[0]
    experts = slot_count * 3 // 8
    tok_rows = tokens.shape[2]
    width = tokens.shape[3]
    chosen_count = expert_ids.shape[3]
    most_rows = (tok_rows * chosen_count + experts - 1) // experts
    capacity = (most_rows + 1) // 2
    buffer_range = jnp.arange(slot_count * capacity, dtype=jnp.int32)
    results = []
    for micro in range(2):
        prepare_rows = tokens[micro, 0]
        normed = normalize(prepare_rows, norm_gain)
        flat = route_rows(expert_ids[micro, 0], placement, experts, capacity)
        hits = flat[:, :, None] == buffer_range[None, None, :]
        take = jnp.any(hits, axis=1).astype(jnp.bfloat16)
        send = lax.dot_general(
            take, normed, (((0,), (0,)), ((), ())), preferred_element_type=jnp.float32
        )
        send = send.astype(jnp.bfloat16).reshape(devices, slot_dev, capacity, width)
        scores = route_scores[micro, 0]
        probs = scores / jnp.sum(scores, axis=1, keepdims=True)
        prepare_mixing = jnp.sum(jnp.where(hits, probs[:, :, None], 0.0), axis=1)
        rows, send, mixing = (prepare_rows, send, prepare_mixing)
        received = lax.all_to_all(send, "expert", split_axis=0, concat_axis=0, tiled=True)
        gate = jnp.einsum("sjcd,jdf->sjcf", received, w_gate, preferred_element_type=jnp.float32)
        up = jnp.einsum("sjcd,jdf->sjcf", received, w_up, preferred_element_type=jnp.float32)
        hidden = (jax.nn.silu(gate) * up).astype(jnp.bfloat16)
        returned = lax.all_to_all(
            jnp.einsum("sjcf,jfd->sjcd", hidden, w_down, preferred_element_type=jnp.float32).astype(
                jnp.bfloat16
            ),
            "expert",
            split_axis=0,
            concat_axis=0,
            tiled=True,
        )
        flat_back = returned.reshape(-1, width).astype(jnp.float32)
        moe = jnp.dot(
            mixing, flat_back, precision=lax.Precision.HIGHEST, preferred_element_type=jnp.float32
        )
        results.append((rows.astype(jnp.float32) + moe).astype(jnp.bfloat16))
    forward = passed_along(results[0], "section", 1)
    backward = passed_along(results[1], "section", -1)
    return jnp.stack([forward, backward], axis=0)[:, None]


def solution(mesh):
    in_specs = (
        P(None, "section", "expert", None),
        P(),
        P(None, "section", "expert", None),
        P(None, "section", "expert", None),
        P(),
        P("expert", None, None),
        P("expert", None, None),
        P("expert", None, None),
    )
    out_specs = P(None, "section", "expert", None)
    return jax.shard_map(body, mesh=mesh, in_specs=in_specs, out_specs=out_specs, check_vma=False)
```

profile of v0, /device:TPU:103, one launch (start us, length us, event | category | flops | bytes accessed | tf_op | source)
XLA Modules:
  0.0 512.7 jit_solution(10610038414811396862)
XLA Ops:
  0.0 0.8 fusion.112
  1.9 0.7 fusion.108
  2.7 0.8 fusion.109
  3.5 0.2 select_reduce_fusion.8
  3.9 0.9 select_reduce_fusion.7
  5.6 1.2 fusion.84
  6.8 2.3 convolution_convert_fusion.1
  9.2 3.3 reshape.169
  12.4 30.4 %all-to-all-start = ((bf16[64,1,3,2048]{3,2,1,0:T(4,128)(2,1)}), bf16[64,1,3,2048]{3,2,1,0:T(4,128)(2,1)}, u32[]{:S(2)}, u32[]{:S(2)}) async-start(bf16[64,1,3,2048]{3,2,1,0:T(4,128)(2,1)} %bitcast.162), calls=%async_computation | async-start | bytes 2097152 | tf_op jit(solution)/shard_map/all_to_all | solution.py:70
  43.6 2.3 convolution_convert_fusion
  45.9 3.3 reshape.176
  49.2 101.7 %all-to-all-done = bf16[64,1,3,2048]{3,2,1,0:T(4,128)(2,1)} async-done(((bf16[64,1,3,2048]{3,2,1,0:T(4,128)(2,1)}), bf16[64,1,3,2048]{3,2,1,0:T(4,128)(2,1)}, u32[]{:S(2)}, u32[]{:S(2)}) %all-to-all-start) | async-done | bytes 786464 | tf_op jit(solution)/shard_map/all_to_all | solution.py:70
  150.9 7.3 %all-to-all-start.2 = ((bf16[64,1,3,2048]{3,2,1,0:T(4,128)(2,1)}), bf16[64,1,3,2048]{3,2,1,0:T(4,128)(2,1)}, u32[]{:S(2)}, u32[]{:S(2)}) async-start(bf16[64,1,3,2048]{3,2,1,0:T(4,128)(2,1)} %bitcast.163), calls=%async_computation.2 | async-start | bytes 2097152 | tf_op jit(solution)/shard_map/all_to_all | solution.py:70
  158.2 4.5 fusion.26
  162.7 5.3 %fusion.21 = bf16[64,1,3,2048]{3,0,2,1:T(8,128)(2,1)} fusion(bf16[1,768,2048]{2,1,0:T(8,128)(2,1)S(1)} %copy-done, bf16[1,2048,768]{2,1,0:T(8,128)(2,1)} %param.14, f32[64,1,3,768]{3,0,2,1:T(8,128)} %fusion.26, bf16[64,1,3,2048]{3,2,1,0:T(4,128)(2,1)} %all-to-all-done), kind=kOutput, calls=%fused_computation.17 | convolution fusion | flops 1209237504 | bytes 8454144 | tf_op jit(solution)/shard_map/sjcf,jfd->sjcd/dot_general | solution.py:75
  168.0 2.8 copy.40
  170.8 95.5 %all-to-all-done.2 = bf16[64,1,3,2048]{3,2,1,0:T(4,128)(2,1)} async-done(((bf16[64,1,3,2048]{3,2,1,0:T(4,128)(2,1)}), bf16[64,1,3,2048]{3,2,1,0:T(4,128)(2,1)}, u32[]{:S(2)}, u32[]{:S(2)}) %all-to-all-start.2) | async-done | bytes 786464 | tf_op jit(solution)/shard_map/all_to_all | solution.py:70
  266.3 7.3 %all-to-all-start.1 = ((bf16[64,1,3,2048]{3,2,1,0:T(4,128)(2,1)}), bf16[64,1,3,2048]{3,2,1,0:T(4,128)(2,1)}, u32[]{:S(2)}, u32[]{:S(2)}) async-start(bf16[64,1,3,2048]{3,2,1,0:T(4,128)(2,1)} %copy.40), calls=%async_computation.1 | async-start | bytes 2097152 | tf_op jit(solution)/shard_map/all_to_all | solution.py:74
  273.6 4.5 fusion.29
  278.1 5.3 %fusion.18 = bf16[64,1,3,2048]{3,0,2,1:T(8,128)(2,1)} fusion(bf16[1,768,2048]{2,1,0:T(8,128)(2,1)S(1)} %copy-done, bf16[1,2048,768]{2,1,0:T(8,128)(2,1)} %param.14, f32[64,1,3,768]{3,0,2,1:T(8,128)} %fusion.29, bf16[64,1,3,2048]{3,2,1,0:T(4,128)(2,1)} %all-to-all-done.2), kind=kOutput, calls=%fused_computation.16 | convolution fusion | flops 1209237504 | bytes 8454144 | tf_op jit(solution)/shard_map/sjcf,jfd->sjcd/dot_general | solution.py:75
  283.4 2.8 copy.45
  286.3 95.4 %all-to-all-done.1 = bf16[64,1,3,2048]{3,2,1,0:T(4,128)(2,1)} async-done(((bf16[64,1,3,2048]{3,2,1,0:T(4,128)(2,1)}), bf16[64,1,3,2048]{3,2,1,0:T(4,128)(2,1)}, u32[]{:S(2)}, u32[]{:S(2)}) %all-to-all-start.1) | async-done | bytes 786464 | tf_op jit(solution)/shard_map/all_to_all | solution.py:74
  381.7 7.3 %all-to-all-start.3 = ((bf16[64,1,3,2048]{3,2,1,0:T(4,128)(2,1)}), bf16[64,1,3,2048]{3,2,1,0:T(4,128)(2,1)}, u32[]{:S(2)}, u32[]{:S(2)}) async-start(bf16[64,1,3,2048]{3,2,1,0:T(4,128)(2,1)} %copy.45), calls=%async_computation.3 | async-start | bytes 2097152 | tf_op jit(solution)/shard_map/all_to_all | solution.py:74
  389.3 3.2 reshape.175
  392.5 2.4 fusion.24
  394.9 3.3 collective-permute-start
  398.2 98.9 %all-to-all-done.3 = bf16[64,1,3,2048]{3,2,1,0:T(4,128)(2,1)} async-done(((bf16[64,1,3,2048]{3,2,1,0:T(4,128)(2,1)}), bf16[64,1,3,2048]{3,2,1,0:T(4,128)(2,1)}, u32[]{:S(2)}, u32[]{:S(2)}) %all-to-all-start.3) | async-done | bytes 786464 | tf_op jit(solution)/shard_map/all_to_all | solution.py:74
  497.1 3.2 reshape.179
  500.3 1.7 fusion.25
  502.0 2.6 collective-permute-start.1
  504.7 7.2 %collective-permute-done.1 = bf16[64,2048]{1,0:T(8,128)(2,1)S(1)} collective-permute-done((bf16[64,2048]{1,0:T(8,128)(2,1)S(1)}, bf16[64,2048]{1,0:T(8,128)(2,1)S(1)}, u32[]{:S(2)}, u32[]{:S(2)}) %collective-permute-start.1) | collective-permute-done | bytes 262176 | tf_op jit(solution)/shard_map/ppermute | solution.py:12
  511.8 0.8 maximum_bitcast_fusion
  (36 shorter events, 3.0 us)
Async XLA Ops:
  0.0 162.7 %copy-start = (bf16[1,768,2048]{2,1,0:T(8,128)(2,1)S(1)}, bf16[1,768,2048]{2,1,0:T(8,128)(2,1)}, u32[]{:S(2)}) copy-start(bf16[1,768,2048]{2,1,0:T(8,128)(2,1)} %param.15) | copy-start | bytes 9437188
  3.8 39.8 %copy-start.1 = (f32[2048]{0:T(1024)S(1)}, f32[2048]{0:T(1024)}, u32[]{:S(2)}) copy-start(f32[2048]{0:T(1024)} %param.9) | copy-start | bytes 24580
  12.4 138.4 %all-to-all-start = ((bf16[64,1,3,2048]{3,2,1,0:T(4,128)(2,1)}), bf16[64,1,3,2048]{3,2,1,0:T(4,128)(2,1)}, u32[]{:S(2)}, u32[]{:S(2)}) async-start(bf16[64,1,3,2048]{3,2,1,0:T(4,128)(2,1)} %bitcast.162), calls=%async_computation | async-start | bytes 2097152 | tf_op jit(solution)/shard_map/all_to_all | solution.py:70
  150.9 115.4 %all-to-all-start.2 = ((bf16[64,1,3,2048]{3,2,1,0:T(4,128)(2,1)}), bf16[64,1,3,2048]{3,2,1,0:T(4,128)(2,1)}, u32[]{:S(2)}, u32[]{:S(2)}) async-start(bf16[64,1,3,2048]{3,2,1,0:T(4,128)(2,1)} %bitcast.163), calls=%async_computation.2 | async-start | bytes 2097152 | tf_op jit(solution)/shard_map/all_to_all | solution.py:70
  266.3 115.4 %all-to-all-start.1 = ((bf16[64,1,3,2048]{3,2,1,0:T(4,128)(2,1)}), bf16[64,1,3,2048]{3,2,1,0:T(4,128)(2,1)}, u32[]{:S(2)}, u32[]{:S(2)}) async-start(bf16[64,1,3,2048]{3,2,1,0:T(4,128)(2,1)} %copy.40), calls=%async_computation.1 | async-start | bytes 2097152 | tf_op jit(solution)/shard_map/all_to_all | solution.py:74
  283.4 105.6 %copy-start.2 = (f32[2,1,64,2]{2,3,1,0:T(2,128)S(1)}, f32[2,1,64,2]{2,3,1,0:T(2,128)}, u32[]{:S(2)}) copy-start(f32[2,1,64,2]{2,3,1,0:T(2,128)} %param.11) | copy-start | bytes 3076
  381.7 115.4 %all-to-all-start.3 = ((bf16[64,1,3,2048]{3,2,1,0:T(4,128)(2,1)}), bf16[64,1,3,2048]{3,2,1,0:T(4,128)(2,1)}, u32[]{:S(2)}, u32[]{:S(2)}) async-start(bf16[64,1,3,2048]{3,2,1,0:T(4,128)(2,1)} %copy.45), calls=%async_computation.3 | async-start | bytes 2097152 | tf_op jit(solution)/shard_map/all_to_all | solution.py:74
  394.9 109.7 %collective-permute-start = (bf16[64,2048]{1,0:T(8,128)(2,1)}, bf16[64,2048]{1,0:T(8,128)(2,1)S(1)}, u32[]{:S(2)}, u32[]{:S(2)}) collective-permute-start(bf16[64,2048]{1,0:T(8,128)(2,1)} %fusion.24), channel_id=1, source_target_pairs={{0,64},{64,128},{128,192},{192,256},{256,320},{320,384},{384,448},... | collective-permute-start | bytes 786440 | tf_op jit(solution)/shard_map/ppermute | solution.py:12
  502.0 9.8 %collective-permute-start.1 = (bf16[64,2048]{1,0:T(8,128)(2,1)S(1)}, bf16[64,2048]{1,0:T(8,128)(2,1)S(1)}, u32[]{:S(2)}, u32[]{:S(2)}) collective-permute-start(bf16[64,2048]{1,0:T(8,128)(2,1)S(1)} %fusion.25), channel_id=1, source_target_pairs={{64,0},{128,64},{192,128},{256,192},{320,256},{384,320},{448,384},... | collective-permute-start | bytes 786440 | tf_op jit(solution)/shard_map/ppermute | solution.py:12
where the time goes:
time: 514 us; the launch traced here: 513 us
  waiting for transfers between devices  399 us (78%)
  starting transfers between devices  58.2 us (11%)
  matrix products  28.4 us (6%)
  local copies, waits for them, and re-layouts  20.3 us (4%)
  other arithmetic  6.8 us (1%)
    all_to_all x2, waiting for transfers between devices, body(): lax.all_to_all(send, 'expert', split_axis=0, concat_axis=0, tiled=True)  197 us
    all_to_all x2, waiting for transfers between devices, body(): lax.all_to_all(jnp.einsum('sjcf,jfd->sjcd', hidden, w_down, preferred_ele...  194 us
    all_to_all x2, starting transfers between devices, body(): lax.all_to_all(send, 'expert', split_axis=0, concat_axis=0, tiled=True)  37.7 us
    all_to_all x2, starting transfers between devices, body(): lax.all_to_all(jnp.einsum('sjcf,jfd->sjcd', hidden, w_down, preferred_ele...  14.6 us
    dot_general x2, matrix products, body(): jnp.einsum('sjcf,jfd->sjcd', hidden, w_down, preferred_element_type=jnp.f...  10.6 us
  transfers between devices with their start and end apart: 6, of which 5 were waited for; matrix products, arithmetic and copies ran while one was open for 8% of the time, Pallas kernels for 0%

commit v1 on v0

--- a/solution.py
+++ b/solution.py
@@ -43,7 +43,6 @@
 
 def body(tokens, norm_gain, expert_ids, route_scores, placement, w_gate, w_up, w_down):
     devices = lax.axis_size("expert")
-    slot_dev = w_gate.shape[0]
     slot_count = placement.shape[0]
     experts = slot_count * 3 // 8
     tok_rows = tokens.shape[2]
@@ -52,39 +51,41 @@
     most_rows = (tok_rows * chosen_count + experts - 1) // experts
     capacity = (most_rows + 1) // 2
     buffer_range = jnp.arange(slot_count * capacity, dtype=jnp.int32)
-    results = []
+    sends = []
+    mixings = []
     for micro in range(2):
-        prepare_rows = tokens[micro, 0]
-        normed = normalize(prepare_rows, norm_gain)
+        normed = normalize(tokens[micro, 0], norm_gain)
         flat = route_rows(expert_ids[micro, 0], placement, experts, capacity)
         hits = flat[:, :, None] == buffer_range[None, None, :]
         take = jnp.any(hits, axis=1).astype(jnp.bfloat16)
         send = lax.dot_general(
             take, normed, (((0,), (0,)), ((), ())), preferred_element_type=jnp.float32
         )
-        send = send.astype(jnp.bfloat16).reshape(devices, slot_dev, capacity, width)
+        sends.append(send.astype(jnp.bfloat16).reshape(devices, capacity, width))
         scores = route_scores[micro, 0]
         probs = scores / jnp.sum(scores, axis=1, keepdims=True)
-        prepare_mixing = jnp.sum(jnp.where(hits, probs[:, :, None], 0.0), axis=1)
-        rows, send, mixing = (prepare_rows, send, prepare_mixing)
-        received = lax.all_to_all(send, "expert", split_axis=0, concat_axis=0, tiled=True)
-        gate = jnp.einsum("sjcd,jdf->sjcf", received, w_gate, preferred_element_type=jnp.float32)
-        up = jnp.einsum("sjcd,jdf->sjcf", received, w_up, preferred_element_type=jnp.float32)
-        hidden = (jax.nn.silu(gate) * up).astype(jnp.bfloat16)
-        returned = lax.all_to_all(
-            jnp.einsum("sjcf,jfd->sjcd", hidden, w_down, preferred_element_type=jnp.float32).astype(
-                jnp.bfloat16
-            ),
-            "expert",
-            split_axis=0,
-            concat_axis=0,
-            tiled=True,
+        mixings.append(jnp.sum(jnp.where(hits, probs[:, :, None], 0.0), axis=1))
+    packed = jnp.stack(sends, axis=1).reshape(devices, -1, 128)
+    received = lax.all_to_all(packed, "expert", split_axis=0, concat_axis=0, tiled=True)
+    received = received.reshape(-1, width)
+    gate = jnp.dot(received, w_gate[0], preferred_element_type=jnp.float32)
+    up = jnp.dot(received, w_up[0], preferred_element_type=jnp.float32)
+    hidden = (jax.nn.silu(gate) * up).astype(jnp.bfloat16)
+    outputs = jnp.dot(hidden, w_down[0], preferred_element_type=jnp.float32).astype(jnp.bfloat16)
+    returned = lax.all_to_all(
+        outputs.reshape(packed.shape), "expert", split_axis=0, concat_axis=0, tiled=True
+    )
+    returned = returned.reshape(devices, 2, capacity, width)
+    results = []
+    for micro in range(2):
+        flat_back = returned[:, micro].reshape(-1, width).astype(jnp.float32)
+        moe = jnp.dot(
+            mixings[micro],
+            flat_back,
+            precision=lax.Precision.HIGHEST,
+            preferred_element_type=jnp.float32,
         )
-        flat_back = returned.reshape(-1, width).astype(jnp.float32)
-        moe = jnp.dot(
-            mixing, flat_back, precision=lax.Precision.HIGHEST, preferred_element_type=jnp.float32
-        )
-        results.append((rows.astype(jnp.float32) + moe).astype(jnp.bfloat16))
+        results.append((tokens[micro, 0].astype(jnp.float32) + moe).astype(jnp.bfloat16))
     forward = passed_along(results[0], "section", 1)
     backward = passed_along(results[1], "section", -1)
     return jnp.stack([forward, backward], axis=0)[:, None]

time: 514 us -> 427 us (0.83)
  waiting for transfers between devices: 399 us -> 160 us
  blocking collectives: 0 us -> 183 us
  starting transfers between devices: 58.2 us -> 13.7 us
  local copies, waits for them, and re-layouts: 20.3 us -> 39.1 us
  matrix products: 28.4 us -> 20.4 us
    all_to_all x4 -> x1, waiting for transfers between devices: 392 us -> 152 us  [body(): lax.all_to_all(outputs.reshape(packed.shape), 'expert', split_axis=0, con...]
    all_to_all x0 -> x1, blocking collectives: none -> 183 us  [body(): lax.all_to_all(packed, 'expert', split_axis=0, concat_axis=0, tiled=True)]
    all_to_all x4 -> x1, starting transfers between devices: 52.3 us -> 8.22 us  [body(): lax.all_to_all(outputs.reshape(packed.shape), 'expert', split_axis=0, con...]
    another operation x0 -> x5, local copies, waits for them, and re-layouts: none -> 15.7 us  [the longest x3 9.28 us: body(): packed = jnp.stack(sends, axis=1).reshape(devices, -1, 128)]
    dot_general x6 -> x4, matrix products: 23.8 us -> 15.8 us  [the longest x1 6.87 us: body(): jnp.dot(hidden, w_down[0], preferred_element_type=jnp.float32)]
    convert_element_type x2 -> x0, local copies, waits for them, and re-layouts: 5.61 us -> none  [body(): jnp.einsum('sjcf,jfd->sjcd', hidden, w_down, preferred_element_type=jnp.f...]
  transfers between devices with their start and end apart: 6 -> 3, of which waited for: 5 -> 2; matrix products, arithmetic and copies ran while one was open for 8% -> 1% of each run, Pallas kernels for 0% -> 0%
where the time goes in v1:
time: 427 us; the launch traced here: 426 us
  blocking collectives  183 us (43%)
  waiting for transfers between devices  160 us (37%)
  local copies, waits for them, and re-layouts  39.1 us (9%)
  matrix products  20.4 us (5%)
  starting transfers between devices  13.7 us (3%)
  other arithmetic  9.91 us (2%)
    all_to_all x1, blocking collectives, body(): lax.all_to_all(packed, 'expert', split_axis=0, concat_axis=0, tiled=True)  183 us
    all_to_all x1, waiting for transfers between devices, body(): lax.all_to_all(outputs.reshape(packed.shape), 'expert', split_axis=0, con...  152 us
    another operation x3, local copies, waits for them, and re-layouts, body(): packed = jnp.stack(sends, axis=1).reshape(devices, -1, 128)  9.28 us
  transfers between devices with their start and end apart: 3, of which 2 were waited for; matrix products, arithmetic and copies ran while one was open for 1% of the time, Pallas kernels for 0%

profile of v1, /device:TPU:103, one launch (start us, length us, event | category | flops | bytes accessed | tf_op | source)
XLA Modules:
  0.0 426.0 jit_solution(5404457260689643109)
XLA Ops:
  0.0 0.9 fusion.46
  1.9 0.7 fusion.42
  2.7 0.8 fusion.43
  3.6 0.2 select_reduce_fusion.8
  3.9 0.9 select_reduce_fusion.7
  4.9 0.2 reduce_window_sum.48
  5.6 1.2 fusion.20
  6.8 2.3 convolution_convert_fusion.1
  9.1 3.3 stack_reshape.6
  12.5 0.2 reduce_window_sum.50
  13.2 2.3 convolution_convert_fusion
  15.5 3.3 stack_reshape.7
  18.8 3.1 pad_maximum_fusion
  21.9 2.7 copy.24
  24.6 5.3 %reshape.135 = bf16[64,96,128]{2,1,0:T(8,128)(2,1)} reshape(bf16[64,2,3,2048]{3,2,1,0:T(4,128)(2,1)} %copy.24) | data formatting | bytes 3145728 | tf_op jit(solution)/shard_map/reshape | solution.py:68
  29.9 182.7 %all_to_all.10 = bf16[64,96,128]{2,1,0:T(8,128)(2,1)} all-to-all(bf16[64,96,128]{2,1,0:T(8,128)(2,1)} %reshape.135), channel_id=1, replica_groups=mesh['section'=16,'expert'=64] {'expert'}, dimensions={0} | all-to-all | bytes 3145728 | tf_op jit(solution)/shard_map/all_to_all | solution.py:69
  212.6 3.7 reshape.136
  216.3 4.8 %fusion.4 = f32[384,768]{1,0:T(8,128)} fusion(bf16[384,2048]{1,0:T(8,128)(2,1)} %reshape.136, bf16[1,2048,768]{2,1,0:T(8,128)(2,1)} %param.13), kind=kOutput, calls=%fused_computation.4 | convolution fusion | flops 1207959552 | bytes 5898240 | tf_op jit(solution)/shard_map/dot_general | solution.py:71
  221.1 6.9 %fusion.6 = bf16[384,2048]{1,0:T(8,128)(2,1)} fusion(bf16[1,768,2048]{2,1,0:T(8,128)(2,1)S(1)} %copy-done, bf16[384,2048]{1,0:T(8,128)(2,1)} %reshape.136, bf16[1,2048,768]{2,1,0:T(8,128)(2,1)} %param.14, f32[384,768]{1,0:T(8,128)} %fusion.4), kind=kOutput, calls=%fused_computation.6 | convolution fusion | flops 2418475008 | bytes 10616832 | tf_op jit(solution)/shard_map/dot_general | solution.py:74
  228.0 3.8 reshape.137
  231.7 8.2 %all-to-all-start.1 = ((bf16[64,96,128]{2,1,0:T(8,128)(2,1)}), bf16[64,96,128]{2,1,0:T(8,128)(2,1)}, u32[]{:S(2)}, u32[]{:S(2)}) async-start(bf16[64,96,128]{2,1,0:T(8,128)(2,1)} %reshape.137), calls=%async_computation.1 | async-start | bytes 3145728 | tf_op jit(solution)/shard_map/all_to_all | solution.py:75
  240.2 152.1 %all-to-all-done.1 = bf16[64,96,128]{2,1,0:T(8,128)(2,1)} async-done(((bf16[64,96,128]{2,1,0:T(8,128)(2,1)}), bf16[64,96,128]{2,1,0:T(8,128)(2,1)}, u32[]{:S(2)}, u32[]{:S(2)}) %all-to-all-start.1) | async-done | bytes 1572896 | tf_op jit(solution)/shard_map/all_to_all | solution.py:75
  392.3 5.1 %reshape.138 = bf16[64,2,3,2048]{3,2,1,0:T(4,128)(2,1)} reshape(bf16[64,96,128]{2,1,0:T(8,128)(2,1)} %all-to-all-done.1) | data formatting | bytes 3145728 | tf_op jit(solution)/shard_map/reshape | solution.py:78
  397.4 3.9 fusion.45
  401.3 3.2 reshape_squeeze.6
  404.4 2.4 fusion.9
  406.9 3.6 collective-permute-start
  410.5 3.2 reshape_squeeze.7
  413.7 1.7 fusion.10
  415.4 1.9 collective-permute-start.1
  417.3 7.9 %collective-permute-done.1 = bf16[64,2048]{1,0:T(8,128)(2,1)S(1)} collective-permute-done((bf16[64,2048]{1,0:T(8,128)(2,1)S(1)}, bf16[64,2048]{1,0:T(8,128)(2,1)S(1)}, u32[]{:S(2)}, u32[]{:S(2)}) %collective-permute-start.1) | collective-permute-done | bytes 262176 | tf_op jit(solution)/shard_map/ppermute | solution.py:12
  425.2 0.8 maximum_bitcast_fusion
  (34 shorter events, 2.6 us)
Async XLA Ops:
  0.0 221.1 %copy-start = (bf16[1,768,2048]{2,1,0:T(8,128)(2,1)S(1)}, bf16[1,768,2048]{2,1,0:T(8,128)(2,1)}, u32[]{:S(2)}) copy-start(bf16[1,768,2048]{2,1,0:T(8,128)(2,1)} %param.15) | copy-start | bytes 9437188
  0.0 6.8 %copy-start.1 = (f32[2048]{0:T(1024)S(1)}, f32[2048]{0:T(1024)}, u32[]{:S(2)}) copy-start(f32[2048]{0:T(1024)} %param.9) | copy-start | bytes 24580
  231.7 8.2 %copy-start.2 = (f32[2,1,64,2]{2,3,1,0:T(2,128)S(1)}, f32[2,1,64,2]{2,3,1,0:T(2,128)}, u32[]{:S(2)}) copy-start(f32[2,1,64,2]{2,3,1,0:T(2,128)} %param.11) | copy-start | bytes 3076
  231.7 160.5 %all-to-all-start.1 = ((bf16[64,96,128]{2,1,0:T(8,128)(2,1)}), bf16[64,96,128]{2,1,0:T(8,128)(2,1)}, u32[]{:S(2)}, u32[]{:S(2)}) async-start(bf16[64,96,128]{2,1,0:T(8,128)(2,1)} %reshape.137), calls=%async_computation.1 | async-start | bytes 3145728 | tf_op jit(solution)/shard_map/all_to_all | solution.py:75
  406.9 10.5 %collective-permute-start = (bf16[64,2048]{1,0:T(8,128)(2,1)}, bf16[64,2048]{1,0:T(8,128)(2,1)S(1)}, u32[]{:S(2)}, u32[]{:S(2)}) collective-permute-start(bf16[64,2048]{1,0:T(8,128)(2,1)} %fusion.9), channel_id=1, source_target_pairs={{0,64},{64,128},{128,192},{192,256},{256,320},{320,384},{384,448},... | collective-permute-start | bytes 786440 | tf_op jit(solution)/shard_map/ppermute | solution.py:12
  415.4 9.8 %collective-permute-start.1 = (bf16[64,2048]{1,0:T(8,128)(2,1)S(1)}, bf16[64,2048]{1,0:T(8,128)(2,1)S(1)}, u32[]{:S(2)}, u32[]{:S(2)}) collective-permute-start(bf16[64,2048]{1,0:T(8,128)(2,1)S(1)} %fusion.10), channel_id=1, source_target_pairs={{64,0},{128,64},{192,128},{256,192},{320,256},{384,320},{448,384},... | collective-permute-start | bytes 786440 | tf_op jit(solution)/shard_map/ppermute | solution.py:12

commit v2 on v1

v2 whole, which is shorter than its diff:
```python
import jax
import jax.numpy as jnp
from jax import lax
from jax.sharding import Mesh
from jax.sharding import PartitionSpec as P

EPSILON = 1e-06
MOST = 6
LANES = 128


def passed_along(x, axis, by):
    peers = lax.axis_size(axis)
    pairs = [(i, i + by) for i in range(peers) if 0 <= i + by < peers]
    return lax.ppermute(x, axis, pairs)


def normalize(rows, gain):
    values = rows.astype(jnp.float32)
    scale = lax.rsqrt(jnp.mean(values * values, axis=-1, keepdims=True) + EPSILON)
    return (values * scale * gain).astype(jnp.bfloat16)


def exclusive_rank(onehot):
    before = jnp.cumsum(onehot, axis=-2) - onehot
    return jnp.sum(before * onehot, axis=-1)


def body(tokens, norm_gain, expert_ids, route_scores, placement, w_gate, w_up, w_down):
    sections = lax.axis_size("section")
    sides = lax.axis_size("side")
    planes = lax.axis_size("plane")
    section = lax.axis_index("section")
    side = lax.axis_index("side")
    plane = lax.axis_index("plane")
    slots = placement.shape[0]
    experts = slots * 3 // 8
    width = tokens.shape[3]
    ff = w_gate.shape[2]
    half_ff = ff // 2
    units = planes // sections
    tok_rows = tokens.shape[2]
    top = expert_ids.shape[3]
    micros = tokens.shape[0]

    expert_range = jnp.arange(experts, dtype=jnp.int32)
    owner = (placement[:, None] == expert_range[None, :]).astype(jnp.int32)
    slot_rank = exclusive_rank(owner)
    slot_range = jnp.arange(slots, dtype=jnp.int32)
    mine = slot_range == side * planes + plane
    half = jnp.sum(jnp.where(mine, slot_rank, 0)) % 2

    k_rows = width // planes
    f_rows = half_ff // units
    blocks = half_ff // LANES

    def piece(number):
        def columns(w):
            part = lax.dynamic_slice(
                w[0], (number * k_rows, half * half_ff), (k_rows, half_ff)
            )
            return part.reshape(k_rows, blocks, LANES).transpose(1, 0, 2)

        down = lax.dynamic_slice(
            w_down[0],
            (half * half_ff + number // sections * f_rows, number % sections * LANES),
            (f_rows, LANES),
        ).reshape(f_rows // k_rows, k_rows, LANES)
        return jnp.concatenate([columns(w_gate), columns(w_up), down], axis=0)

    unit = plane // sections

    def hand_over(flip):
        pairs = []
        for q in range(sections):
            for j in range(planes):
                u = j // sections
                target = q + sections * (1 - u if flip else u)
                pairs.append((q * planes + j, j % sections * planes + target))
        target = section + sections * (1 - unit if flip else unit)
        return lax.ppermute(piece(target), ("section", "plane"), pairs)

    same = hand_over(False)
    other = hand_over(True)
    low = plane < sections
    share = jnp.concatenate(
        [jnp.where(low, same, other), jnp.where(low, other, same)], axis=0
    )
    gathered = lax.all_gather(share, "plane", axis=0)
    weights = gathered.transpose(1, 0, 2, 3)
    per_unit = share.shape[0] // units

    def column_weights(first):
        chosen = [
            weights[u * per_unit + first + b].reshape(width, LANES)
            for u in range(units)
            for b in range(blocks)
        ]
        return jnp.concatenate(chosen, axis=1)

    gate_all = column_weights(0)
    up_all = column_weights(blocks)
    down_all = weights.reshape(units, per_unit, units, sections, k_rows, LANES)[:, 2 * blocks :]
    down_all = down_all.transpose(0, 2, 1, 4, 3, 5).reshape(ff, width)

    per_slot = micros * MOST
    per_host = units * per_slot
    slot_side = slot_range // planes
    slot_plane = slot_range % planes
    slot_base = (
        slot_plane % sections * sides + slot_side
    ) * per_host + slot_plane // sections * per_slot
    bases = [
        jnp.sum(jnp.where(slot_rank == h, slot_base, 0)[:, None] * owner, axis=0) for h in range(2)
    ]
    ids = expert_ids[:, 0].reshape(micros, tok_rows * top)
    hit = (ids[:, :, None] == expert_range).astype(jnp.int32)
    rank = exclusive_rank(hit) + MOST * jnp.arange(micros, dtype=jnp.int32)[:, None]
    scores = route_scores[:, 0]
    probs = scores / jnp.sum(scores, axis=-1, keepdims=True)
    total = sections * sides * per_host
    buffer_range = jnp.arange(total, dtype=jnp.int32)
    take = jnp.zeros((micros * tok_rows, total), jnp.float32)
    mixing = jnp.zeros((micros * tok_rows, total), jnp.float32)
    for base in bases:
        index = (jnp.sum(hit * base, axis=-1) + rank).reshape(micros * tok_rows, top)
        for k in range(top):
            at = index[:, k : k + 1] == buffer_range
            take = jnp.where(at, 1.0, take)
            mixing = jnp.where(at, probs[:, :, k].reshape(-1, 1), mixing)

    normed = normalize(tokens[:, 0].reshape(micros * tok_rows, width), norm_gain)
    send = lax.dot_general(
        take.astype(jnp.bfloat16),
        normed,
        (((0,), (0,)), ((), ())),
        preferred_element_type=jnp.float32,
    ).astype(jnp.bfloat16)
    hosts = sections * sides

    def exchange(x):
        x = x.reshape(hosts, per_host, width)
        x = lax.all_to_all(x, ("section", "side"), split_axis=0, concat_axis=0, tiled=True)
        return x.reshape(total, width)

    received = exchange(send)
    gate = jnp.dot(received, gate_all, preferred_element_type=jnp.float32)
    up = jnp.dot(received, up_all, preferred_element_type=jnp.float32)
    row_unit = jnp.arange(total, dtype=jnp.int32) % per_host // per_slot
    column_unit = jnp.arange(ff, dtype=jnp.int32) // half_ff
    own = row_unit[:, None] == column_unit[None, :]
    hidden = jnp.where(own, jax.nn.silu(gate) * up, 0.0).astype(jnp.bfloat16)
    partial = jnp.dot(hidden, down_all, preferred_element_type=jnp.float32).astype(jnp.bfloat16)
    returned = exchange(partial)
    moe = jnp.dot(
        mixing,
        returned.astype(jnp.float32),
        precision=lax.Precision.HIGHEST,
        preferred_element_type=jnp.float32,
    )
    mixed = tokens[:, 0].astype(jnp.float32) + moe.reshape(micros, tok_rows, width)
    mixed = mixed.astype(jnp.bfloat16)
    forward = passed_along(mixed[0], "section", 1)
    backward = passed_along(mixed[1], "section", -1)
    return jnp.stack([forward, backward], axis=0)[:, None]


def solution(mesh):
    sections, devices = mesh.devices.shape
    planes = devices // 2
    grid = Mesh(mesh.devices.reshape(sections, 2, planes), ("section", "side", "plane"))
    where = ("side", "plane")
    in_specs = (
        P(None, "section", where, None),
        P(),
        P(None, "section", where, None),
        P(None, "section", where, None),
        P(),
        P(where, None, None),
        P(where, None, None),
        P(where, None, None),
    )
    out_specs = P(None, "section", where, None)
    return jax.shard_map(body, mesh=grid, in_specs=in_specs, out_specs=out_specs, check_vma=False)
```

time: 427 us -> 396 us (0.927)
  the two profiles are of different devices: /device:TPU:103 before, /device:TPU:8 now
where the time goes in v2:
time: 396 us; the launch traced here: 395 us
  waiting for transfers between devices  228 us (58%)
  starting transfers between devices  89.8 us (23%)
  local copies, waits for them, and re-layouts  33.6 us (8%)
  matrix products  22.9 us (6%)
  between operations  15.8 us (4%)
  other arithmetic  4.94 us (1%)
    all_gather x1, waiting for transfers between devices, body(): gathered = lax.all_gather(share, 'plane', axis=0)  131 us
    all_to_all x2, starting transfers between devices, exchange(): lax.all_to_all(x, ('section', 'side'), split_axis=0, concat_axis=0, tiled...  50.7 us
    ppermute x2, waiting for transfers between devices, hand_over(): return lax.ppermute(piece(target), ('section', 'plane'), pairs)  50.6 us
    all_to_all x2, waiting for transfers between devices, exchange(): lax.all_to_all(x, ('section', 'side'), split_axis=0, concat_axis=0, tiled...  38.4 us
    ppermute x2, starting transfers between devices, hand_over(): return lax.ppermute(piece(target), ('section', 'plane'), pairs)  32.3 us
    dot_general x1, matrix products, body(): jnp.dot(hidden, down_all, preferred_element_type=jnp.float32)  11.4 us
    transpose x1, local copies, waits for them, and re-layouts, body(): weights = gathered.transpose(1, 0, 2, 3)  10.7 us
    unnamed x37, local copies, waits for them, and re-layouts  8.28 us
  transfers between devices with their start and end apart: 7, of which 6 were waited for; matrix products, arithmetic and copies ran while one was open for 8% of the time, Pallas kernels for 0%

profile of v2, /device:TPU:8, one launch (start us, length us, event | category | flops | bytes accessed | tf_op | source)
XLA Modules:
  0.0 395.4 jit_solution(12366101775124040838)
XLA Ops:
  7.4 0.8 select_reduce_fusion.5
  11.0 0.8 constant_dynamic-slice_fusion.3
  11.9 0.9 constant_dynamic-slice_fusion.4
  13.0 15.6 %collective-permute-start = (bf16[9,64,128]{2,0,1:T(8,128)(2,1)S(1)}, bf16[9,64,128]{2,0,1:T(8,128)(2,1)S(1)}, u32[]{:S(2)}, u32[]{:S(2)}) collective-permute-start(bf16[9,64,128]{2,0,1:T(8,128)(2,1)S(1)} %pad_maximum_fusion.1), channel_id=1, source_target_pairs={{0,0},{1,64},{2,128},{3,192},{4,256},{5,320},{6,384},{7,448},{8,51... | collective-permute-start | bytes 442376 | tf_op jit(solution)/shard_map/ppermute | solution.py:81
  28.9 16.7 %collective-permute-start.1 = (bf16[9,64,128]{2,0,1:T(8,128)(2,1)S(1)}, bf16[9,64,128]{2,0,1:T(8,128)(2,1)S(1)}, u32[]{:S(2)}, u32[]{:S(2)}) collective-permute-start(bf16[9,64,128]{2,0,1:T(8,128)(2,1)S(1)} %pad_maximum_fusion.2), channel_id=1, source_target_pairs={{0,16},{1,80},{2,144},{3,208},{4,272},{5,336},{6,400},{7,464},{8,5... | collective-permute-start | bytes 442376 | tf_op jit(solution)/shard_map/ppermute | solution.py:81
  45.7 35.1 %collective-permute-done = bf16[9,64,128]{2,0,1:T(8,128)(2,1)S(1)} collective-permute-done((bf16[9,64,128]{2,0,1:T(8,128)(2,1)S(1)}, bf16[9,64,128]{2,0,1:T(8,128)(2,1)S(1)}, u32[]{:S(2)}, u32[]{:S(2)}) %collective-permute-start) | collective-permute-done | bytes 147488 | tf_op jit(solution)/shard_map/ppermute | solution.py:81
  80.8 15.4 %collective-permute-done.1 = bf16[9,64,128]{2,0,1:T(8,128)(2,1)S(1)} collective-permute-done((bf16[9,64,128]{2,0,1:T(8,128)(2,1)S(1)}, bf16[9,64,128]{2,0,1:T(8,128)(2,1)S(1)}, u32[]{:S(2)}, u32[]{:S(2)}) %collective-permute-start.1) | collective-permute-done | bytes 147488 | tf_op jit(solution)/shard_map/ppermute | solution.py:81
  99.6 2.8 convolution_convert_fusion.1
  102.5 43.0 %all-to-all-start = ((bf16[32,24,2048]{2,1,0:T(8,128)(2,1)}), bf16[32,24,2048]{2,1,0:T(8,128)(2,1)S(1)}, u32[]{:S(2)}, u32[]{:S(2)}) async-start(bf16[32,24,2048]{2,1,0:T(8,128)(2,1)} %bitcast.7), calls=%async_computation | async-start | bytes 6291456 | tf_op jit(solution)/shard_map/all_to_all | solution.py:143
  145.5 131.4 %all-gather.3.cloned.1.call-done = bf16[576,64,128]{2,1,0:T(8,128)(2,1)} async-done(((bf16[18,64,128]{2,1,0:T(8,128)(2,1)}), bf16[576,64,128]{2,1,0:T(8,128)(2,1)}) %all-gather.3.cloned.1.call-update) | async-done | bytes 9437200 | tf_op jit(solution)/shard_map/all_gather | solution.py:89
  276.9 10.7 %copy.27 = bf16[18,32,64,128]{3,2,1,0:T(8,128)(2,1)} copy(bf16[18,32,64,128]{3,2,0,1:T(8,128)(2,1)} %bitcast.76) | data formatting | bytes 18874368 | tf_op jit(solution)/shard_map/transpose | solution.py:90
  287.6 2.8 slice_bitcast_fusion
  290.4 4.1 %copy.28 = bf16[2,2,3,64,16,128]{5,4,3,2,1,0:T(8,128)(2,1)} copy(bf16[2,2,3,64,16,128]{5,3,4,1,2,0:T(8,128)(2,1)S(1)} %slice_bitcast_fusion) | data formatting | bytes 6291456 | tf_op jit(solution)/shard_map/transpose | solution.py:104
  294.5 2.7 fusion.42
  297.2 0.9 constant_dynamic-update-slice_fusion.5
  298.1 0.9 constant_dynamic-update-slice_fusion.11
  299.0 0.9 constant_dynamic-update-slice_fusion.4
  299.9 0.8 constant_dynamic-update-slice_fusion.3
  300.8 0.9 constant_dynamic-update-slice_fusion.2
  301.6 0.9 constant_dynamic-update-slice_fusion.1
  302.5 0.9 constant_dynamic-update-slice_fusion
  303.5 6.1 %fusion.44 = f32[768,768]{1,0:T(8,128)} fusion(bf16[768,2048]{1,0:T(8,128)(2,1)S(1)} %bitcast.79, bf16[2048,768]{1,0:T(8,128)(2,1)} %constant_dynamic-update-slice_fusion), kind=kOutput, calls=%fused_computation.126 | convolution fusion | flops 2415919104 | bytes 8650752 | tf_op jit(solution)/shard_map/dot_general | solution.py:147
  310.9 1.7 copy-done.8
  312.5 11.4 %convolution_convert_fusion = bf16[768,2048]{1,0:T(8,128)(2,1)} fusion(bf16[96,8,16,128]{3,2,1,0:T(8,128)(2,1)} %bitcast.81, f32[768,768]{1,0:T(8,128)} %fusion.44, bf16[768,2048]{1,0:T(8,128)(2,1)S(1)} %bitcast.80, bf16[2048,768]{1,0:T(8,128)(2,1)} %copy-done.8, s32[768]{0:T(1024)S(1)} %get-tuple-element.47, s32[768]{0:T(1024)S(1)} %get-tuple-element.48), kind=kOutput, calls=%fused_computation | convolution fusion | flops 4838129664 | bytes 14948352 | tf_op jit(solution)/shard_map/dot_general | solution.py:153
  323.9 7.7 %all-to-all-start.1 = ((bf16[32,24,2048]{2,1,0:T(8,128)(2,1)}), bf16[32,24,2048]{2,1,0:T(8,128)(2,1)S(1)}, u32[]{:S(2)}, u32[]{:S(2)}) async-start(bf16[32,24,2048]{2,1,0:T(8,128)(2,1)} %bitcast.82), calls=%async_computation.1 | async-start | bytes 6291456 | tf_op jit(solution)/shard_map/all_to_all | solution.py:143
  332.0 38.4 %all-to-all-done.1 = bf16[32,24,2048]{2,1,0:T(8,128)(2,1)S(1)} async-done(((bf16[32,24,2048]{2,1,0:T(8,128)(2,1)}), bf16[32,24,2048]{2,1,0:T(8,128)(2,1)S(1)}, u32[]{:S(2)}, u32[]{:S(2)}) %all-to-all-start.1) | async-done | bytes 3145760 | tf_op jit(solution)/shard_map/all_to_all | solution.py:143
  370.3 2.6 fusion.2
  373.0 4.9 %collective-permute-start.3 = (bf16[64,2048]{1,0:T(8,128)(2,1)S(1)}, bf16[64,2048]{1,0:T(8,128)(2,1)S(1)}, u32[]{:S(2)}, u32[]{:S(2)}) collective-permute-start(bf16[64,2048]{1,0:T(8,128)(2,1)S(1)} %get-tuple-element.33), channel_id=1, source_target_pairs={{64,0},{128,64},{192,128},{256,192},{320,256},{384,320},{448,384},... | collective-permute-start | bytes 786440 | tf_op jit(solution)/shard_map/ppermute | solution.py:15
  377.9 1.9 collective-permute-start.2
  379.8 1.9 collective-permute-done.3
  381.8 5.9 %collective-permute-done.2 = bf16[64,2048]{1,0:T(8,128)(2,1)S(1)} collective-permute-done((bf16[64,2048]{1,0:T(8,128)(2,1)S(1)}, bf16[64,2048]{1,0:T(8,128)(2,1)S(1)}, u32[]{:S(2)}, u32[]{:S(2)}) %collective-permute-start.2) | collective-permute-done | bytes 262176 | tf_op jit(solution)/shard_map/ppermute | solution.py:15
  387.7 0.8 maximum_bitcast_fusion
  (75 shorter events, 7.0 us)
Async XLA Ops:
  6.5 90.7 %copy-start.1 = (bf16[2,1,64,2048]{3,2,1,0:T(8,128)(2,1)S(1)}, bf16[2,1,64,2048]{3,2,1,0:T(8,128)(2,1)}, u32[]{:S(2)}) copy-start(bf16[2,1,64,2048]{3,2,1,0:T(8,128)(2,1)} %param.8) | copy-start | bytes 1572868
  6.5 91.0 %copy-start.12 = (s32[2,1,64,2]{2,3,1,0:T(2,128)S(1)}, s32[2,1,64,2]{2,3,1,0:T(2,128)}, u32[]{:S(2)}) copy-start(s32[2,1,64,2]{2,3,1,0:T(2,128)} %param.10) | copy-start | bytes 3076
  6.5 270.4 %all-gather.3.cloned.1.call-start = ((), (), s32[]{:S(2)}) async-start(), calls=%async_computation.2 | async-start | bytes 9732096 | tf_op jit(solution)/shard_map/all_gather | solution.py:89
  10.9 87.2 %copy-start.11 = (s32[64]{0:T(128)S(1)}, s32[64]{0:T(128)}, u32[]{:S(2)}) copy-start(s32[64]{0:T(128)} %param.12) | copy-start | bytes 772
  13.0 67.8 %collective-permute-start = (bf16[9,64,128]{2,0,1:T(8,128)(2,1)S(1)}, bf16[9,64,128]{2,0,1:T(8,128)(2,1)S(1)}, u32[]{:S(2)}, u32[]{:S(2)}) collective-permute-start(bf16[9,64,128]{2,0,1:T(8,128)(2,1)S(1)} %pad_maximum_fusion.1), channel_id=1, source_target_pairs={{0,0},{1,64},{2,128},{3,192},{4,256},{5,320},{6,384},{7,448},{8,51... | collective-permute-start | bytes 442376 | tf_op jit(solution)/shard_map/ppermute | solution.py:81
  28.9 67.3 %collective-permute-start.1 = (bf16[9,64,128]{2,0,1:T(8,128)(2,1)S(1)}, bf16[9,64,128]{2,0,1:T(8,128)(2,1)S(1)}, u32[]{:S(2)}, u32[]{:S(2)}) collective-permute-start(bf16[9,64,128]{2,0,1:T(8,128)(2,1)S(1)} %pad_maximum_fusion.2), channel_id=1, source_target_pairs={{0,16},{1,80},{2,144},{3,208},{4,272},{5,336},{6,400},{7,464},{8,5... | collective-permute-start | bytes 442376 | tf_op jit(solution)/shard_map/ppermute | solution.py:81
  45.7 53.8 %copy-start.9 = (f32[2048]{0:T(1024)S(1)}, f32[2048]{0:T(1024)}, u32[]{:S(2)}) copy-start(f32[2048]{0:T(1024)} %param.9) | copy-start | bytes 24580
  102.5 201.0 %all-to-all-start = ((bf16[32,24,2048]{2,1,0:T(8,128)(2,1)}), bf16[32,24,2048]{2,1,0:T(8,128)(2,1)S(1)}, u32[]{:S(2)}, u32[]{:S(2)}) async-start(bf16[32,24,2048]{2,1,0:T(8,128)(2,1)} %bitcast.7), calls=%async_computation | async-start | bytes 6291456 | tf_op jit(solution)/shard_map/all_to_all | solution.py:143
  287.6 6.9 %copy-start = (bf16[576,64,128]{2,1,0:T(8,128)(2,1)S(1)}, bf16[576,64,128]{2,1,0:T(8,128)(2,1)}, u32[]{:S(2)}) copy-start(bf16[576,64,128]{2,1,0:T(8,128)(2,1)} %all-gather.3.cloned.1.call-done) | copy-start | bytes 28311556
  303.5 6.1 %copy-start.6 = (bf16[1,32,64,128]{3,2,0,1:T(8,128)(2,1)S(1)}, bf16[1,32,64,128]{3,2,0,1:T(8,128)(2,1)}, u32[]{:S(2)}) copy-start(bf16[1,32,64,128]{3,2,0,1:T(8,128)(2,1)} %get-tuple-element.18) | copy-start | bytes 1572868
  303.5 6.1 %copy-start.7 = (bf16[2048,768]{1,0:T(8,128)(2,1)S(1)}, bf16[2048,768]{1,0:T(8,128)(2,1)}, u32[]{:S(2)}) copy-start(bf16[2048,768]{1,0:T(8,128)(2,1)} %constant_dynamic-update-slice_fusion.11) | copy-start | bytes 9437188
  303.5 6.2 %copy-start.5 = (bf16[1,32,64,128]{3,2,0,1:T(8,128)(2,1)S(1)}, bf16[1,32,64,128]{3,2,0,1:T(8,128)(2,1)}, u32[]{:S(2)}) copy-start(bf16[1,32,64,128]{3,2,0,1:T(8,128)(2,1)} %get-tuple-element.17) | copy-start | bytes 1572868
  303.5 6.4 %copy-start.4 = (bf16[1,32,64,128]{3,2,0,1:T(8,128)(2,1)S(1)}, bf16[1,32,64,128]{3,2,0,1:T(8,128)(2,1)}, u32[]{:S(2)}) copy-start(bf16[1,32,64,128]{3,2,0,1:T(8,128)(2,1)} %get-tuple-element.16) | copy-start | bytes 1572868
  309.5 1.0 copy-start.3
  309.5 1.2 copy-start.2
  310.9 1.7 copy-start.8
  323.9 8.0 %copy-start.10 = (f32[2,1,64,2]{2,3,1,0:T(2,128)S(1)}, f32[2,1,64,2]{2,3,1,0:T(2,128)}, u32[]{:S(2)}) copy-start(f32[2,1,64,2]{2,3,1,0:T(2,128)} %param.11) | copy-start | bytes 3076
  323.9 46.4 %all-to-all-start.1 = ((bf16[32,24,2048]{2,1,0:T(8,128)(2,1)}), bf16[32,24,2048]{2,1,0:T(8,128)(2,1)S(1)}, u32[]{:S(2)}, u32[]{:S(2)}) async-start(bf16[32,24,2048]{2,1,0:T(8,128)(2,1)} %bitcast.82), calls=%async_computation.1 | async-start | bytes 6291456 | tf_op jit(solution)/shard_map/all_to_all | solution.py:143
  373.0 8.8 %collective-permute-start.3 = (bf16[64,2048]{1,0:T(8,128)(2,1)S(1)}, bf16[64,2048]{1,0:T(8,128)(2,1)S(1)}, u32[]{:S(2)}, u32[]{:S(2)}) collective-permute-start(bf16[64,2048]{1,0:T(8,128)(2,1)S(1)} %get-tuple-element.33), channel_id=1, source_target_pairs={{64,0},{128,64},{192,128},{256,192},{320,256},{384,320},{448,384},... | collective-permute-start | bytes 786440 | tf_op jit(solution)/shard_map/ppermute | solution.py:15
  377.9 9.8 %collective-permute-start.2 = (bf16[64,2048]{1,0:T(8,128)(2,1)S(1)}, bf16[64,2048]{1,0:T(8,128)(2,1)S(1)}, u32[]{:S(2)}, u32[]{:S(2)}) collective-permute-start(bf16[64,2048]{1,0:T(8,128)(2,1)S(1)} %get-tuple-element.32), channel_id=1, source_target_pairs={{0,64},{64,128},{128,192},{192,256},{256,320},{320,384},{384,448},... | collective-permute-start | bytes 786440 | tf_op jit(solution)/shard_map/ppermute | solution.py:15
Sparse Core Ops, SparseCore 0:
  97.3 179.5 all-gather.2

commit v3 on v2

--- a/solution.py
+++ b/solution.py
@@ -1,6 +1,10 @@
+import functools
+
 import jax
 import jax.numpy as jnp
 from jax import lax
+from jax.experimental import pallas as pl
+from jax.experimental.pallas import tpu as pltpu
 from jax.sharding import Mesh
 from jax.sharding import PartitionSpec as P
 
@@ -24,6 +28,91 @@
 def exclusive_rank(onehot):
     before = jnp.cumsum(onehot, axis=-2) - onehot
     return jnp.sum(before * onehot, axis=-1)
+
+
+def expert_kernel(units, blocks, per_slot, rows_in, gathered, out, weights, hidden, sem):
+    planes, _, k_rows, _ = gathered.shape
+    total, width = rows_in.shape
+    count = weights.shape[0]
+    per_unit = count // units
+    sections = planes // units
+
+    def copy(index):
+        return pltpu.make_async_copy(gathered.at[:, index], weights.at[index], sem.at[index])
+
+    order = [u * per_unit + part * blocks + b for part in range(3) for u in range(units) for b in range(blocks)]
+    for index in order:
+        copy(index).start()
+
+    step = total // 3
+    for pair in range(0, units * blocks, 2):
+        columns = [(c // blocks, c % blocks) for c in (pair, pair + 1)]
+        at = [u * per_unit + b for u, b in columns]
+        for index in at:
+            copy(index).wait()
+            copy(index + blocks).wait()
+
+        def load(offset):
+            return jnp.concatenate(
+                [weights[index + offset].reshape(width, LANES) for index in at], axis=1
+            )
+
+        @pl.loop(0, total // step)
+        def _(i):
+            rows = pl.ds(pl.multiple_of(i * step, 16), step)
+            x = rows_in[rows, :]
+            gate = jnp.dot(x, load(0), preferred_element_type=jnp.float32)
+            up = jnp.dot(x, load(blocks), preferred_element_type=jnp.float32)
+            value = gate / (1.0 + jnp.exp(-gate)) * up
+            row = lax.broadcasted_iota(jnp.int32, value.shape, 0) + i * step
+            column = lax.broadcasted_iota(jnp.int32, value.shape, 1)
+            row_unit = row // per_slot % units
+            column_unit = jnp.where(column < LANES, columns[0][0], columns[1][0])
+            value = jnp.where(row_unit == column_unit, value, 0.0)
+            hidden[rows, pair * LANES : (pair + 2) * LANES] = value.astype(jnp.bfloat16)
+
+    for u in range(units):
+        for b in range(blocks):
+            copy(u * per_unit + 2 * blocks + b).wait()
+    for first in range(0, sections, 2):
+
+        def down(b):
+            parts = [
+                weights[u * per_unit + 2 * blocks + i, a * sections + b]
+                for u in range(units)
+                for a in range(units)
+                for i in range(blocks)
+            ]
+            return jnp.concatenate(parts, axis=0)
+
+        w = jnp.concatenate([down(first), down(first + 1)], axis=1)
+        out[:, first * LANES : (first + 2) * LANES] = jnp.dot(
+            hidden[...], w, preferred_element_type=jnp.float32
+        ).astype(jnp.bfloat16)
+
+
+def run_experts(received, gathered, units, blocks, per_slot, ff):
+    total, width = received.shape
+    vmem = pl.BlockSpec(memory_space=pltpu.VMEM)
+    count = gathered.shape[1]
+    shape = (count, gathered.shape[0]) + gathered.shape[2:]
+    return pl.pallas_call(
+        functools.partial(expert_kernel, units, blocks, per_slot),
+        out_shape=jax.ShapeDtypeStruct((total, width), jnp.bfloat16),
+        in_specs=[vmem, pl.BlockSpec(memory_space=pl.ANY)],
+        out_specs=vmem,
+        scratch_shapes=[
+            pltpu.VMEM(shape, jnp.bfloat16),
+            pltpu.VMEM((total, ff), jnp.bfloat16),
+            pltpu.SemaphoreType.DMA((count,)),
+        ],
+        cost_estimate=pl.CostEstimate(
+            flops=6 * total * width * ff,
+            bytes_accessed=2 * gathered.size + 4 * total * width,
+            transcendentals=total * ff,
+        ),
+        compiler_params=pltpu.CompilerParams(vmem_limit_bytes=40 << 20),
+    )(received, gathered)
 
 
 def body(tokens, norm_gain, expert_ids, route_scores, placement, w_gate, w_up, w_down):
@@ -68,41 +157,41 @@
         ).reshape(f_rows // k_rows, k_rows, LANES)
         return jnp.concatenate([columns(w_gate), columns(w_up), down], axis=0)
 
-    unit = plane // sections
-
-    def hand_over(flip):
-        pairs = []
-        for q in range(sections):
-            for j in range(planes):
-                u = j // sections
-                target = q + sections * (1 - u if flip else u)
-                pairs.append((q * planes + j, j % sections * planes + target))
-        target = section + sections * (1 - unit if flip else unit)
-        return lax.ppermute(piece(target), ("section", "plane"), pairs)
-
-    same = hand_over(False)
-    other = hand_over(True)
-    low = plane < sections
+    def offset_of(q):
+        return q // 2 if q % 2 == 0 else (sections - q // 2 if q > 1 else sections // 2)
+
+    offsets = [offset_of(q) for q in range(sections)]
+    pair = section // 2
+    odd = jnp.where(pair == 0, sections // 2, sections - pair)
+    offset = jnp.where(section % 2 == 0, pair, odd)
+    arrived = []
+    for i in range(units):
+        number = (plane + offset + i * sections) % planes
+        moves = [
+            (q * planes + j, q * planes + (j + offsets[q] + i * sections) % planes)
+            for q in range(sections)
+            for j in range(planes)
+        ]
+        arrived.append(lax.ppermute(piece(number), ("section", "plane"), moves))
+    moves = [
+        (q * planes + m, (m - offsets[q]) % sections * planes + m)
+        for q in range(sections)
+        for m in range(planes)
+    ]
+    share = lax.ppermute(jnp.stack(arrived), ("section", "plane"), moves)
+    first = (plane - (plane - section) % sections) % planes // sections
     share = jnp.concatenate(
-        [jnp.where(low, same, other), jnp.where(low, other, same)], axis=0
+        [
+            functools.reduce(
+                lambda x, i: jnp.where(first == i, share[(u - i) % units], x),
+                range(1, units),
+                share[u],
+            )
+            for u in range(units)
+        ],
+        axis=0,
     )
     gathered = lax.all_gather(share, "plane", axis=0)
-    weights = gathered.transpose(1, 0, 2, 3)
-    per_unit = share.shape[0] // units
-
-    def column_weights(first):
-        chosen = [
-            weights[u * per_unit + first + b].reshape(width, LANES)
-            for u in range(units)
-            for b in range(blocks)
-        ]
-        return jnp.concatenate(chosen, axis=1)
-
-    gate_all = column_weights(0)
-    up_all = column_weights(blocks)
-    down_all = weights.reshape(units, per_unit, units, sections, k_rows, LANES)[:, 2 * blocks :]
-    down_all = down_all.transpose(0, 2, 1, 4, 3, 5).reshape(ff, width)
-
     per_slot = micros * MOST
     per_host = units * per_slot
     slot_side = slot_range // planes
@@ -144,13 +233,7 @@
         return x.reshape(total, width)
 
     received = exchange(send)
-    gate = jnp.dot(received, gate_all, preferred_element_type=jnp.float32)
-    up = jnp.dot(received, up_all, preferred_element_type=jnp.float32)
-    row_unit = jnp.arange(total, dtype=jnp.int32) % per_host // per_slot
-    column_unit = jnp.arange(ff, dtype=jnp.int32) // half_ff
-    own = row_unit[:, None] == column_unit[None, :]
-    hidden = jnp.where(own, jax.nn.silu(gate) * up, 0.0).astype(jnp.bfloat16)
-    partial = jnp.dot(hidden, down_all, preferred_element_type=jnp.float32).astype(jnp.bfloat16)
+    partial = run_experts(received, gathered, units, blocks, per_slot, ff)
     returned = exchange(partial)
     moe = jnp.dot(
         mixing,

time: 396 us -> 342 us (0.86)
  blocking collectives: 0 us -> 53.4 us
  waiting for transfers between devices: 228 us -> 187 us
  starting transfers between devices: 89.8 us -> 58.8 us
  local copies, waits for them, and re-layouts: 33.6 us -> 4.25 us
  matrix products: 22.9 us -> 3.76 us
  Pallas kernels: 0 us -> 13.8 us
    all_to_all x0 -> x1, blocking collectives: none -> 53.4 us  [exchange(): lax.all_to_all(x, ('section', 'side'), split_axis=0, concat_axis=0, tiled...]
    all_to_all x2 -> x1, starting transfers between devices: 50.7 us -> 7.56 us  [exchange(): lax.all_to_all(x, ('section', 'side'), split_axis=0, concat_axis=0, tiled...]
    all_gather x1, waiting for transfers between devices: 131 us -> 93.6 us  [body(): gathered = lax.all_gather(share, 'plane', axis=0)]
    transpose x3 -> x0, local copies, waits for them, and re-layouts: 17.6 us -> none  [the longest x1 10.7 us: body(): weights = gathered.transpose(1, 0, 2, 3)]
    dot_general x2 -> x0, matrix products: 17.4 us -> none  [the longest x1 11.4 us: body(): jnp.dot(hidden, down_all, preferred_element_type=jnp.float32)]
    pallas_call x0 -> x1, Pallas kernels: none -> 13.8 us  [run_experts(): pl.pallas_call(functools.partial(expert_kernel, units, blocks, per_slot),...]
    ppermute x2 -> x3, starting transfers between devices: 32.3 us -> 44.4 us  [the longest x2 30.3 us: body(): arrived.append(lax.ppermute(piece(number), ('section', 'plane'), moves))]
    unnamed x37 -> x11, local copies, waits for them, and re-layouts: 8.28 us -> 0.14 us
  transfers between devices with their start and end apart: 7 -> 7, of which waited for: 6 -> 7; matrix products, arithmetic and copies ran while one was open for 8% -> 1% of each run, Pallas kernels for 0% -> 0%
where the time goes in v3:
time: 342 us
  waiting for transfers between devices  187 us (55%)
  starting transfers between devices  58.8 us (17%)
  blocking collectives  53.4 us (16%)
  between operations  15.9 us (5%)
  Pallas kernels  13.8 us (4%)
  other arithmetic  4.97 us (1%)
  local copies, waits for them, and re-layouts  4.25 us (1%)
  matrix products  3.76 us (1%)
    all_gather x1, waiting for transfers between devices, body(): gathered = lax.all_gather(share, 'plane', axis=0)  93.6 us
    all_to_all x1, blocking collectives, exchange(): lax.all_to_all(x, ('section', 'side'), split_axis=0, concat_axis=0, tiled...  53.4 us
    all_to_all x1, waiting for transfers between devices, exchange(): lax.all_to_all(x, ('section', 'side'), split_axis=0, concat_axis=0, tiled...  38.4 us
    ppermute x2, waiting for transfers between devices, body(): arrived.append(lax.ppermute(piece(number), ('section', 'plane'), moves))  35.7 us
    ppermute x2, starting transfers between devices, body(): arrived.append(lax.ppermute(piece(number), ('section', 'plane'), moves))  30.3 us
    ppermute x1, starting transfers between devices, body(): share = lax.ppermute(jnp.stack(arrived), ('section', 'plane'), moves)  14.2 us
    pallas_call x1, Pallas kernels, run_experts(): pl.pallas_call(functools.partial(expert_kernel, units, blocks, per_slot),...  13.8 us
    ppermute x1, waiting for transfers between devices, body(): share = lax.ppermute(jnp.stack(arrived), ('section', 'plane'), moves)  11.3 us
  transfers between devices with their start and end apart: 7, of which 7 were waited for; matrix products, arithmetic and copies ran while one was open for 1% of the time, Pallas kernels for 0%

profile of v3, /device:TPU:8, one launch (start us, length us, event | category | flops | bytes accessed | tf_op | source)
XLA Modules:
  0.0 341.8 jit_solution(17507054242863549871)
XLA Ops:
  6.5 0.7 fusion.22
  7.4 0.8 select_reduce_fusion.5
  8.2 0.6 fusion.27
  11.0 0.9 constant_dynamic-slice_fusion.3
  11.9 0.9 constant_dynamic-slice_fusion.4
  12.9 0.2 pad_maximum_fusion.3
  13.1 26.0 %collective-permute-start.1 = (bf16[9,64,128]{2,0,1:T(8,128)(2,1)S(1)}, bf16[9,64,128]{2,0,1:T(8,128)(2,1)S(1)}, u32[]{:S(2)}, u32[]{:S(2)}) collective-permute-start(bf16[9,64,128]{2,0,1:T(8,128)(2,1)S(1)} %pad_maximum_fusion.3), channel_id=1, source_target_pairs={{0,16},{1,17},{2,18},{3,19},{4,20},{5,21},{6,22},{7,23},{8,24},{9,... | collective-permute-start | bytes 442376 | tf_op jit(solution)/shard_map/ppermute | solution.py:175
  39.2 0.2 pad_maximum_fusion.2
  39.3 4.3 %collective-permute-start = (bf16[9,64,128]{2,0,1:T(8,128)(2,1)S(1)}, bf16[9,64,128]{2,0,1:T(8,128)(2,1)S(1)}, u32[]{:S(2)}, u32[]{:S(2)}) collective-permute-start(bf16[9,64,128]{2,0,1:T(8,128)(2,1)S(1)} %pad_maximum_fusion.2), channel_id=1, source_target_pairs={{0,0},{1,1},{2,2},{3,3},{4,4},{5,5},{6,6},{7,7},{8,8},{9,9},{10,10... | collective-permute-start | bytes 442376 | tf_op jit(solution)/shard_map/ppermute | solution.py:175
  43.6 34.7 %collective-permute-done.1 = bf16[9,64,128]{2,0,1:T(8,128)(2,1)S(1)} collective-permute-done((bf16[9,64,128]{2,0,1:T(8,128)(2,1)S(1)}, bf16[9,64,128]{2,0,1:T(8,128)(2,1)S(1)}, u32[]{:S(2)}, u32[]{:S(2)}) %collective-permute-start.1) | collective-permute-done | bytes 147488 | tf_op jit(solution)/shard_map/ppermute | solution.py:175
  78.4 1.0 collective-permute-done
  79.5 14.2 %collective-permute-start.2 = (bf16[2,9,64,128]{3,1,2,0:T(8,128)(2,1)S(1)}, bf16[2,9,64,128]{3,1,2,0:T(8,128)(2,1)S(1)}, u32[]{:S(2)}, u32[]{:S(2)}) collective-permute-start(bf16[2,9,64,128]{3,1,2,0:T(8,128)(2,1)S(1)} %pad_maximum_fusion), channel_id=1, source_target_pairs={{0,0},{1,65},{2,130},{3,195},{4,260},{5,325},{6,390},{7,455},{8,52... | collective-permute-start | bytes 884744 | tf_op jit(solution)/shard_map/ppermute | solution.py:181
  93.7 11.3 %collective-permute-done.2 = bf16[2,9,64,128]{3,1,2,0:T(8,128)(2,1)S(1)} collective-permute-done((bf16[2,9,64,128]{3,1,2,0:T(8,128)(2,1)S(1)}, bf16[2,9,64,128]{3,1,2,0:T(8,128)(2,1)S(1)}, u32[]{:S(2)}, u32[]{:S(2)}) %collective-permute-start.2) | collective-permute-done | bytes 294944 | tf_op jit(solution)/shard_map/ppermute | solution.py:181
  105.2 0.8 copy.25
  106.0 0.2 multiply_reduce_fusion
  106.4 0.1 eq.222
  106.6 0.2 reduce_window_sum.23
  106.9 0.3 select_reduce_fusion.2
  107.9 0.2 slice_reduce_fusion.1
  108.2 0.2 fusion.2
  108.4 1.2 convolution_convert_fusion
  109.5 53.4 %all_to_all.10 = bf16[32,24,2048]{2,1,0:T(8,128)(2,1)S(1)} all-to-all(bf16[32,24,2048]{2,1,0:T(8,128)(2,1)S(1)} %bitcast.57), channel_id=1, replica_groups=mesh['section'=16,'side'=2,'plane'=32] {'section','side'}, dimensions={0} | all-to-all | bytes 6291456 | tf_op jit(solution)/shard_map/all_to_all | solution.py:232
  163.0 93.6 %all-gather.3.cloned.1.call-done = bf16[576,64,128]{2,1,0:T(8,128)(2,1)} async-done(((bf16[18,64,128]{2,1,0:T(8,128)(2,1)}), bf16[576,64,128]{2,1,0:T(8,128)(2,1)}) %all-gather.3.cloned.1.call-update) | async-done | bytes 9437200 | tf_op jit(solution)/shard_map/all_gather | solution.py:194
  256.6 13.8 %shard_map.82 = bf16[768,2048]{1,0:T(8,128)(2,1)} custom-call(bf16[768,2048]{1,0:T(8,128)(2,1)S(1)} %bitcast.56, bf16[32,18,64,128]{3,2,1,0:T(8,128)(2,1)} %bitcast.71), custom_call_target="tpu_custom_call" | custom-call | flops 7247757312 | bytes 15728640 | tf_op jit(solution)/shard_map/pallas_call | solution.py:99
  270.4 7.6 %all-to-all-start.1 = ((bf16[32,24,2048]{2,1,0:T(8,128)(2,1)}), bf16[32,24,2048]{2,1,0:T(8,128)(2,1)S(1)}, u32[]{:S(2)}, u32[]{:S(2)}) async-start(bf16[32,24,2048]{2,1,0:T(8,128)(2,1)} %bitcast.20), calls=%async_computation.1 | async-start | bytes 6291456 | tf_op jit(solution)/shard_map/all_to_all | solution.py:232
  278.4 38.4 %all-to-all-done.1 = bf16[32,24,2048]{2,1,0:T(8,128)(2,1)S(1)} async-done(((bf16[32,24,2048]{2,1,0:T(8,128)(2,1)}), bf16[32,24,2048]{2,1,0:T(8,128)(2,1)S(1)}, u32[]{:S(2)}, u32[]{:S(2)}) %all-to-all-start.1) | async-done | bytes 3145760 | tf_op jit(solution)/shard_map/all_to_all | solution.py:232
  316.7 2.6 fusion
  319.4 4.9 %collective-permute-start.4 = (bf16[64,2048]{1,0:T(8,128)(2,1)S(1)}, bf16[64,2048]{1,0:T(8,128)(2,1)S(1)}, u32[]{:S(2)}, u32[]{:S(2)}) collective-permute-start(bf16[64,2048]{1,0:T(8,128)(2,1)S(1)} %get-tuple-element.21), channel_id=1, source_target_pairs={{64,0},{128,64},{192,128},{256,192},{320,256},{384,320},{448,384},... | collective-permute-start | bytes 786440 | tf_op jit(solution)/shard_map/ppermute | solution.py:19
  324.3 1.9 collective-permute-start.3
  326.2 1.9 collective-permute-done.4
  328.1 5.9 %collective-permute-done.3 = bf16[64,2048]{1,0:T(8,128)(2,1)S(1)} collective-permute-done((bf16[64,2048]{1,0:T(8,128)(2,1)S(1)}, bf16[64,2048]{1,0:T(8,128)(2,1)S(1)}, u32[]{:S(2)}, u32[]{:S(2)}) %collective-permute-start.3) | collective-permute-done | bytes 262176 | tf_op jit(solution)/shard_map/ppermute | solution.py:19
  334.1 0.8 maximum_bitcast_fusion
  (43 shorter events, 2.2 us)
Async XLA Ops:
  6.5 250.0 %all-gather.3.cloned.1.call-start = ((), (), s32[]{:S(2)}) async-start(), calls=%async_computation.2 | async-start | bytes 9732096 | tf_op jit(solution)/shard_map/all_gather | solution.py:194
  10.9 95.0 %copy-start = (bf16[2,1,64,2048]{3,2,1,0:T(8,128)(2,1)S(1)}, bf16[2,1,64,2048]{3,2,1,0:T(8,128)(2,1)}, u32[]{:S(2)}) copy-start(bf16[2,1,64,2048]{3,2,1,0:T(8,128)(2,1)} %param.8) | copy-start | bytes 1572868
  12.8 93.4 %copy-start.4 = (s32[2,1,64,2]{2,3,1,0:T(2,128)S(1)}, s32[2,1,64,2]{2,3,1,0:T(2,128)}, u32[]{:S(2)}) copy-start(s32[2,1,64,2]{2,3,1,0:T(2,128)} %param.10) | copy-start | bytes 3076
  12.9 93.9 %copy-start.3 = (s32[64]{0:T(128)S(1)}, s32[64]{0:T(128)}, u32[]{:S(2)}) copy-start(s32[64]{0:T(128)} %param.12) | copy-start | bytes 772
  13.1 65.3 %collective-permute-start.1 = (bf16[9,64,128]{2,0,1:T(8,128)(2,1)S(1)}, bf16[9,64,128]{2,0,1:T(8,128)(2,1)S(1)}, u32[]{:S(2)}, u32[]{:S(2)}) collective-permute-start(bf16[9,64,128]{2,0,1:T(8,128)(2,1)S(1)} %pad_maximum_fusion.3), channel_id=1, source_target_pairs={{0,16},{1,17},{2,18},{3,19},{4,20},{5,21},{6,22},{7,23},{8,24},{9,... | collective-permute-start | bytes 442376 | tf_op jit(solution)/shard_map/ppermute | solution.py:175
  39.3 40.0 %collective-permute-start = (bf16[9,64,128]{2,0,1:T(8,128)(2,1)S(1)}, bf16[9,64,128]{2,0,1:T(8,128)(2,1)S(1)}, u32[]{:S(2)}, u32[]{:S(2)}) collective-permute-start(bf16[9,64,128]{2,0,1:T(8,128)(2,1)S(1)} %pad_maximum_fusion.2), channel_id=1, source_target_pairs={{0,0},{1,1},{2,2},{3,3},{4,4},{5,5},{6,6},{7,7},{8,8},{9,9},{10,10... | collective-permute-start | bytes 442376 | tf_op jit(solution)/shard_map/ppermute | solution.py:175
  79.5 25.5 %collective-permute-start.2 = (bf16[2,9,64,128]{3,1,2,0:T(8,128)(2,1)S(1)}, bf16[2,9,64,128]{3,1,2,0:T(8,128)(2,1)S(1)}, u32[]{:S(2)}, u32[]{:S(2)}) collective-permute-start(bf16[2,9,64,128]{3,1,2,0:T(8,128)(2,1)S(1)} %pad_maximum_fusion), channel_id=1, source_target_pairs={{0,0},{1,65},{2,130},{3,195},{4,260},{5,325},{6,390},{7,455},{8,52... | collective-permute-start | bytes 884744 | tf_op jit(solution)/shard_map/ppermute | solution.py:181
  93.7 14.5 %copy-start.1 = (f32[2048]{0:T(1024)S(1)}, f32[2048]{0:T(1024)}, u32[]{:S(2)}) copy-start(f32[2048]{0:T(1024)} %param.9) | copy-start | bytes 24580
  270.4 7.9 %copy-start.2 = (f32[2,1,64,2]{2,3,1,0:T(2,128)S(1)}, f32[2,1,64,2]{2,3,1,0:T(2,128)}, u32[]{:S(2)}) copy-start(f32[2,1,64,2]{2,3,1,0:T(2,128)} %param.11) | copy-start | bytes 3076
  270.4 46.3 %all-to-all-start.1 = ((bf16[32,24,2048]{2,1,0:T(8,128)(2,1)}), bf16[32,24,2048]{2,1,0:T(8,128)(2,1)S(1)}, u32[]{:S(2)}, u32[]{:S(2)}) async-start(bf16[32,24,2048]{2,1,0:T(8,128)(2,1)} %bitcast.20), calls=%async_computation.1 | async-start | bytes 6291456 | tf_op jit(solution)/shard_map/all_to_all | solution.py:232
  319.4 8.8 %collective-permute-start.4 = (bf16[64,2048]{1,0:T(8,128)(2,1)S(1)}, bf16[64,2048]{1,0:T(8,128)(2,1)S(1)}, u32[]{:S(2)}, u32[]{:S(2)}) collective-permute-start(bf16[64,2048]{1,0:T(8,128)(2,1)S(1)} %get-tuple-element.21), channel_id=1, source_target_pairs={{64,0},{128,64},{192,128},{256,192},{320,256},{384,320},{448,384},... | collective-permute-start | bytes 786440 | tf_op jit(solution)/shard_map/ppermute | solution.py:19
  324.3 9.8 %collective-permute-start.3 = (bf16[64,2048]{1,0:T(8,128)(2,1)S(1)}, bf16[64,2048]{1,0:T(8,128)(2,1)S(1)}, u32[]{:S(2)}, u32[]{:S(2)}) collective-permute-start(bf16[64,2048]{1,0:T(8,128)(2,1)S(1)} %get-tuple-element.20), channel_id=1, source_target_pairs={{0,64},{64,128},{128,192},{192,256},{256,320},{320,384},{384,448},... | collective-permute-start | bytes 786440 | tf_op jit(solution)/shard_map/ppermute | solution.py:19
Sparse Core Ops, SparseCore 0:
  106.1 150.4 all-gather.2

commit v4 on v3

--- a/solution.py
+++ b/solution.py
@@ -30,27 +30,40 @@
     return jnp.sum(before * onehot, axis=-1)
 
 
-def expert_kernel(units, blocks, per_slot, rows_in, gathered, out, weights, hidden, sem):
-    planes, _, k_rows, _ = gathered.shape
+def expert_kernel(units, blocks, per_slot, place, rows_in, gathered, out, weights, hidden, sems):
+    planes = gathered.shape[0]
+    k_rows = gathered.shape[3]
     total, width = rows_in.shape
-    count = weights.shape[0]
-    per_unit = count // units
+    per_unit = gathered.shape[1]
     sections = planes // units
 
-    def copy(index):
-        return pltpu.make_async_copy(gathered.at[:, index], weights.at[index], sem.at[index])
-
-    order = [u * per_unit + part * blocks + b for part in range(3) for u in range(units) for b in range(blocks)]
-    for index in order:
-        copy(index).start()
-
+    def copies(part, u):
+        home = place[0] + u * sections
+        for r in range(sections):
+            shift = lax.rem(r - home + planes + sections // 2, sections)
+            m = lax.rem(home + planes - sections // 2 + shift, planes)
+            yield pltpu.make_async_copy(
+                gathered.at[m, pl.ds(part * blocks, blocks)],
+                weights.at[pl.ds(u * per_unit + part * blocks, blocks), :, r],
+                sems.at[part, u, r],
+            )
+
+    for part in range(3):
+        for u in range(units):
+            for copy in copies(part, u):
+                copy.start()
+
+    def arrive(part, u):
+        for copy in copies(part, u):
+            copy.wait()
+
+    for part in range(2):
+        for u in range(units):
+            arrive(part, u)
     step = total // 3
     for pair in range(0, units * blocks, 2):
         columns = [(c // blocks, c % blocks) for c in (pair, pair + 1)]
         at = [u * per_unit + b for u, b in columns]
-        for index in at:
-            copy(index).wait()
-            copy(index + blocks).wait()
 
         def load(offset):
             return jnp.concatenate(
@@ -72,15 +85,14 @@
             hidden[rows, pair * LANES : (pair + 2) * LANES] = value.astype(jnp.bfloat16)
 
     for u in range(units):
-        for b in range(blocks):
-            copy(u * per_unit + 2 * blocks + b).wait()
+        arrive(2, u)
     for first in range(0, sections, 2):
 
         def down(b):
             parts = [
-                weights[u * per_unit + 2 * blocks + i, a * sections + b]
+                weights[u * per_unit + 2 * blocks + i, a, b]
                 for u in range(units)
-                for a in range(units)
+                for a in range(2)
                 for i in range(blocks)
             ]
             return jnp.concatenate(parts, axis=0)
@@ -91,20 +103,24 @@
         ).astype(jnp.bfloat16)
 
 
-def run_experts(received, gathered, units, blocks, per_slot, ff):
+def run_experts(received, gathered, place, units, blocks, per_slot, ff):
     total, width = received.shape
     vmem = pl.BlockSpec(memory_space=pltpu.VMEM)
-    count = gathered.shape[1]
-    shape = (count, gathered.shape[0]) + gathered.shape[2:]
+    planes, per_unit, pieces, k_rows, lanes = gathered.shape
+    shape = (units * per_unit, pieces, planes // units, k_rows, lanes)
     return pl.pallas_call(
         functools.partial(expert_kernel, units, blocks, per_slot),
         out_shape=jax.ShapeDtypeStruct((total, width), jnp.bfloat16),
-        in_specs=[vmem, pl.BlockSpec(memory_space=pl.ANY)],
+        in_specs=[
+            pl.BlockSpec(memory_space=pltpu.SMEM),
+            vmem,
+            pl.BlockSpec(memory_space=pl.ANY),
+        ],
         out_specs=vmem,
         scratch_shapes=[
             pltpu.VMEM(shape, jnp.bfloat16),
             pltpu.VMEM((total, ff), jnp.bfloat16),
-            pltpu.SemaphoreType.DMA((count,)),
+            pltpu.SemaphoreType.DMA((3, units, planes // units)),
         ],
         cost_estimate=pl.CostEstimate(
             flops=6 * total * width * ff,
@@ -112,7 +128,7 @@
             transcendentals=total * ff,
         ),
         compiler_params=pltpu.CompilerParams(vmem_limit_bytes=40 << 20),
-    )(received, gathered)
+    )(place, received, gathered)
 
 
 def body(tokens, norm_gain, expert_ids, route_scores, placement, w_gate, w_up, w_down):
@@ -157,40 +173,48 @@
         ).reshape(f_rows // k_rows, k_rows, LANES)
         return jnp.concatenate([columns(w_gate), columns(w_up), down], axis=0)
 
-    def offset_of(q):
-        return q // 2 if q % 2 == 0 else (sections - q // 2 if q > 1 else sections // 2)
-
-    offsets = [offset_of(q) for q in range(sections)]
-    pair = section // 2
-    odd = jnp.where(pair == 0, sections // 2, sections - pair)
-    offset = jnp.where(section % 2 == 0, pair, odd)
+    quarter = sections // 4
+
+    def distance(q, i):
+        step = q // 2 % quarter
+        back = (step - sections // 2) if q % 2 == 0 else -1 - step
+        ahead = (sections // 2 - 1 - step) if q % 2 == 0 else step
+        return back if (q // 2 < quarter) == (i == 0) else ahead
+
+    def my_distance(i):
+        step = section // 2 % quarter
+        even = section % 2 == 0
+        back = jnp.where(even, step - sections // 2, -1 - step)
+        ahead = jnp.where(even, sections // 2 - 1 - step, step)
+        return jnp.where((section // 2 < quarter) == (i == 0), back, ahead)
+
     arrived = []
-    for i in range(units):
-        number = (plane + offset + i * sections) % planes
+    for i in range(2):
+        target = (plane + my_distance(i)) % planes
+        number = i * sections + target % sections
         moves = [
-            (q * planes + j, q * planes + (j + offsets[q] + i * sections) % planes)
+            (q * planes + j, q * planes + (j + distance(q, i)) % planes)
             for q in range(sections)
             for j in range(planes)
         ]
         arrived.append(lax.ppermute(piece(number), ("section", "plane"), moves))
-    moves = [
-        (q * planes + m, (m - offsets[q]) % sections * planes + m)
-        for q in range(sections)
-        for m in range(planes)
-    ]
-    share = lax.ppermute(jnp.stack(arrived), ("section", "plane"), moves)
-    first = (plane - (plane - section) % sections) % planes // sections
-    share = jnp.concatenate(
-        [
-            functools.reduce(
-                lambda x, i: jnp.where(first == i, share[(u - i) % units], x),
-                range(1, units),
-                share[u],
-            )
-            for u in range(units)
-        ],
-        axis=0,
-    )
+    for i in range(2):
+        moves = [
+            (q * planes + m, (m - distance(q, i)) % sections * planes + m)
+            for q in range(sections)
+            for m in range(planes)
+        ]
+        arrived[i] = lax.ppermute(arrived[i], ("section", "plane"), moves)
+    share = jnp.stack(arrived, axis=1)
+
+    routing = jnp.concatenate([expert_ids[:, 0].astype(jnp.float32), route_scores[:, 0]], axis=-1)
+    share, tokens, routing = lax.optimization_barrier((share, tokens, routing))
+    ways = (1, -1)
+    tokens = jnp.stack([passed_along(tokens[m, 0], "section", ways[m]) for m in range(micros)])
+    routing = jnp.stack([passed_along(routing[m], "section", ways[m]) for m in range(micros)])
+    filled = jnp.stack([section > 0, section < sections - 1])
+    expert_ids = routing[:, :, :top].astype(jnp.int32)
+    scores = routing[:, :, top:]
     gathered = lax.all_gather(share, "plane", axis=0)
     per_slot = micros * MOST
     per_host = units * per_slot
@@ -202,11 +226,11 @@
     bases = [
         jnp.sum(jnp.where(slot_rank == h, slot_base, 0)[:, None] * owner, axis=0) for h in range(2)
     ]
-    ids = expert_ids[:, 0].reshape(micros, tok_rows * top)
+    ids = expert_ids.reshape(micros, tok_rows * top)
     hit = (ids[:, :, None] == expert_range).astype(jnp.int32)
     rank = exclusive_rank(hit) + MOST * jnp.arange(micros, dtype=jnp.int32)[:, None]
-    scores = route_scores[:, 0]
     probs = scores / jnp.sum(scores, axis=-1, keepdims=True)
+    probs = jnp.where(filled[:, None, None], probs, 0.0)
     total = sections * sides * per_host
     buffer_range = jnp.arange(total, dtype=jnp.int32)
     take = jnp.zeros((micros * tok_rows, total), jnp.float32)
@@ -218,7 +242,7 @@
             take = jnp.where(at, 1.0, take)
             mixing = jnp.where(at, probs[:, :, k].reshape(-1, 1), mixing)
 
-    normed = normalize(tokens[:, 0].reshape(micros * tok_rows, width), norm_gain)
+    normed = normalize(tokens.reshape(micros * tok_rows, width), norm_gain)
     send = lax.dot_general(
         take.astype(jnp.bfloat16),
         normed,
@@ -233,7 +257,8 @@
         return x.reshape(total, width)
 
     received = exchange(send)
-    partial = run_experts(received, gathered, units, blocks, per_slot, ff)
+    place = jnp.full((1,), section, jnp.int32)
+    partial = run_experts(received, gathered, place, units, blocks, per_slot, ff)
     returned = exchange(partial)
     moe = jnp.dot(
         mixing,
@@ -241,11 +266,9 @@
         precision=lax.Precision.HIGHEST,
         preferred_element_type=jnp.float32,
     )
-    mixed = tokens[:, 0].astype(jnp.float32) + moe.reshape(micros, tok_rows, width)
-    mixed = mixed.astype(jnp.bfloat16)
-    forward = passed_along(mixed[0], "section", 1)
-    backward = passed_along(mixed[1], "section", -1)
-    return jnp.stack([forward, backward], axis=0)[:, None]
+    mixed = tokens.astype(jnp.float32) + moe.reshape(micros, tok_rows, width)
+    mixed = jnp.where(filled[:, None, None], mixed, 0.0)
+    return mixed.astype(jnp.bfloat16)[:, None]
 
 
 def solution(mesh):

time: 342 us -> 300 us (0.88)
  the two profiles are of different devices: /device:TPU:8 before, /device:TPU:2 now
where the time goes in v4:
time: 300 us
  waiting for transfers between devices  151 us (50%)
  starting transfers between devices  52.2 us (17%)
  blocking collectives  51.2 us (17%)
  between operations  15.8 us (5%)
  Pallas kernels  15.3 us (5%)
  other arithmetic  5.52 us (2%)
  matrix products  4.48 us (1%)
  local copies, waits for them, and re-layouts  4.36 us (1%)
    all_gather x1, waiting for transfers between devices, body(): gathered = lax.all_gather(share, 'plane', axis=0)  84.1 us
    all_to_all x1, blocking collectives, exchange(): lax.all_to_all(x, ('section', 'side'), split_axis=0, concat_axis=0, tiled...  51.2 us
    all_to_all x1, waiting for transfers between devices, exchange(): lax.all_to_all(x, ('section', 'side'), split_axis=0, concat_axis=0, tiled...  42.6 us
    ppermute x2, starting transfers between devices, body(): arrived.append(lax.ppermute(piece(number), ('section', 'plane'), moves))  27.8 us
    ppermute x2, waiting for transfers between devices, body(): arrived.append(lax.ppermute(piece(number), ('section', 'plane'), moves))  16.3 us
    pallas_call x1, Pallas kernels, run_experts(): pl.pallas_call(functools.partial(expert_kernel, units, blocks, per_slot),...  15.3 us
    ppermute x4, starting transfers between devices, passed_along(): return lax.ppermute(x, axis, pairs)  11.1 us
    all_to_all x1, starting transfers between devices, exchange(): lax.all_to_all(x, ('section', 'side'), split_axis=0, concat_axis=0, tiled...  7.08 us
  transfers between devices with their start and end apart: 10, of which 7 were waited for; matrix products, arithmetic and copies ran while one was open for 2% of the time, Pallas kernels for 0%

profile of v4, /device:TPU:2, one launch (start us, length us, event | category | flops | bytes accessed | tf_op | source)
XLA Modules:
  0.0 299.6 jit_solution(4014509181146657265)
XLA Ops:
  6.5 0.8 fusion.24
  7.4 0.8 select_reduce_fusion.5
  8.3 0.6 compare_select_fusion
  10.9 0.9 constant_dynamic-slice_fusion.4
  11.9 0.8 constant_dynamic-slice_fusion.3
  13.0 22.6 %collective-permute-start = (bf16[9,64,128]{2,0,1:T(8,128)(2,1)S(1)}, bf16[9,64,128]{2,0,1:T(8,128)(2,1)S(1)}, u32[]{:S(2)}, u32[]{:S(2)}) collective-permute-start(bf16[9,64,128]{2,0,1:T(8,128)(2,1)S(1)} %pad_maximum_fusion.1), channel_id=1, source_target_pairs={{0,24},{1,25},{2,26},{3,27},{4,28},{5,29},{6,30},{7,31},{8,0},{9,1... | collective-permute-start | bytes 442376 | tf_op jit(solution)/shard_map/ppermute | solution.py:200
  35.8 5.2 %collective-permute-start.2 = (bf16[9,64,128]{2,0,1:T(8,128)(2,1)S(1)}, bf16[9,64,128]{2,0,1:T(8,128)(2,1)S(1)}, u32[]{:S(2)}, u32[]{:S(2)}) collective-permute-start(bf16[9,64,128]{2,0,1:T(8,128)(2,1)S(1)} %pad_maximum_fusion.2), channel_id=1, source_target_pairs={{0,7},{1,8},{2,9},{3,10},{4,11},{5,12},{6,13},{7,14},{8,15},{9,16}... | collective-permute-start | bytes 442376 | tf_op jit(solution)/shard_map/ppermute | solution.py:200
  41.0 16.3 %collective-permute-done = bf16[9,64,128]{2,0,1:T(8,128)(2,1)S(1)} collective-permute-done((bf16[9,64,128]{2,0,1:T(8,128)(2,1)S(1)}, bf16[9,64,128]{2,0,1:T(8,128)(2,1)S(1)}, u32[]{:S(2)}, u32[]{:S(2)}) %collective-permute-start) | collective-permute-done | bytes 147488 | tf_op jit(solution)/shard_map/ppermute | solution.py:200
  57.4 4.0 %collective-permute-start.1 = (bf16[9,64,128]{2,0,1:T(8,128)(2,1)S(1)}, bf16[9,64,128]{2,0,1:T(8,128)(2,1)S(1)}, u32[]{:S(2)}, u32[]{:S(2)}) collective-permute-start(bf16[9,64,128]{2,0,1:T(8,128)(2,1)S(1)} %collective-permute-done), channel_id=1, source_target_pairs={{0,512},{1,577},{2,642},{3,707},{4,772},{5,837},{6,902},{7,967},{8... | collective-permute-start | bytes 442376 | tf_op jit(solution)/shard_map/ppermute | solution.py:207
  61.4 2.2 collective-permute-start.3
  63.6 0.7 fusion.27
  64.3 0.7 pad_maximum_fusion.3
  65.0 0.3 collective-permute-done.1
  65.3 5.5 %collective-permute-done.3 = bf16[9,64,128]{2,0,1:T(8,128)(2,1)S(1)} collective-permute-done((bf16[9,64,128]{2,0,1:T(8,128)(2,1)S(1)}, bf16[9,64,128]{2,0,1:T(8,128)(2,1)S(1)}, u32[]{:S(2)}, u32[]{:S(2)}) %collective-permute-start.3) | collective-permute-done | bytes 147488 | tf_op jit(solution)/shard_map/ppermute | solution.py:207
  70.9 0.8 copy.25
  72.1 1.9 collective-permute-start.6
  74.0 3.6 %collective-permute-start.7 = (f32[64,4]{0,1:T(4,128)S(1)}, f32[64,4]{0,1:T(4,128)S(1)}, u32[]{:S(2)}, u32[]{:S(2)}) collective-permute-start(f32[64,4]{0,1:T(4,128)S(1)} %get-tuple-element.32), channel_id=1, source_target_pairs={{64,0},{128,64},{192,128},{256,192},{320,256},{384,320},{448,384},... | collective-permute-start | bytes 3080 | tf_op jit(solution)/shard_map/ppermute | solution.py:19
  77.7 3.1 %collective-permute-start.4 = (bf16[64,2048]{1,0:T(8,128)(2,1)S(1)}, bf16[64,2048]{1,0:T(8,128)(2,1)S(1)}, u32[]{:S(2)}, u32[]{:S(2)}) collective-permute-start(bf16[64,2048]{1,0:T(8,128)(2,1)S(1)} %get-tuple-element.26), channel_id=1, source_target_pairs={{0,64},{64,128},{128,192},{192,256},{256,320},{320,384},{384,448},... | collective-permute-start | bytes 786440 | tf_op jit(solution)/shard_map/ppermute | solution.py:19
  80.9 2.4 collective-permute-start.5
  83.8 0.2 reduce_window_sum.23
  84.0 0.2 select_reduce_fusion.2
  85.0 0.2 slice_reduce_fusion.1
  85.1 0.3 collective-permute-done.4
  85.4 1.8 collective-permute-done.5
  87.2 0.2 multiply_reduce_fusion
  87.7 1.1 convolution_convert_fusion
  88.9 51.2 %all_to_all.10 = bf16[32,24,2048]{2,1,0:T(8,128)(2,1)S(1)} all-to-all(bf16[32,24,2048]{2,1,0:T(8,128)(2,1)S(1)} %bitcast.55), channel_id=1, replica_groups=mesh['section'=16,'side'=2,'plane'=32] {'section','side'}, dimensions={0} | all-to-all | bytes 6291456 | tf_op jit(solution)/shard_map/all_to_all | solution.py:256
  140.1 84.1 %all-gather.3.cloned.1.call-done = bf16[288,2,64,128]{3,2,1,0:T(8,128)(2,1)} async-done(((bf16[9,2,64,128]{3,2,1,0:T(8,128)(2,1)}), bf16[288,2,64,128]{3,2,1,0:T(8,128)(2,1)}) %all-gather.3.cloned.1.call-update) | async-done | bytes 9437200 | tf_op jit(solution)/shard_map/all_gather | solution.py:218
  224.1 15.3 %shard_map.82 = bf16[768,2048]{1,0:T(8,128)(2,1)} custom-call(s32[1]{0:T(128)} %bitcast.24.place, bf16[768,2048]{1,0:T(8,128)(2,1)S(1)} %bitcast.54, bf16[32,9,2,64,128]{4,3,2,1,0:T(8,128)(2,1)} %bitcast.78), custom_call_target="tpu_custom_call" | custom-call | flops 7247757312 | bytes 15728640 | tf_op jit(solution)/shard_map/pallas_call | solution.py:111
  239.4 7.1 %all-to-all-start.1 = ((bf16[32,24,2048]{2,1,0:T(8,128)(2,1)}), bf16[32,24,2048]{2,1,0:T(8,128)(2,1)S(1)}, u32[]{:S(2)}, u32[]{:S(2)}) async-start(bf16[32,24,2048]{2,1,0:T(8,128)(2,1)} %bitcast.29), calls=%async_computation.1 | async-start | bytes 6291456 | tf_op jit(solution)/shard_map/all_to_all | solution.py:256
  246.8 42.6 %all-to-all-done.1 = bf16[32,24,2048]{2,1,0:T(8,128)(2,1)S(1)} async-done(((bf16[32,24,2048]{2,1,0:T(8,128)(2,1)}), bf16[32,24,2048]{2,1,0:T(8,128)(2,1)S(1)}, u32[]{:S(2)}, u32[]{:S(2)}) %all-to-all-start.1) | async-done | bytes 3145760 | tf_op jit(solution)/shard_map/all_to_all | solution.py:256
  289.4 3.3 %fusion.2 = bf16[2,1,64,2048]{3,2,1,0:T(8,128)(2,1)} fusion(bf16[768,2048,1]{1,0,2:T(8,128)(2,1)S(1)} %bitcast.56, pred[2]{0:T(512)(128)(4,1)S(1)} %pad_add_fusion, s32[2,64]{1,0:T(2,128)S(1)} %eq.248, s32[2,64]{1,0:T(2,128)S(1)} %eq.244, f32[2,64]{1,0:T(2,128)S(1)} %bitcast.77, s32[2,64]{1,0:T(2,128)S(1)} %eq.239, f32[2,64]{1,0:T(2,128)S(1)} %bitcast.76, ...), kind=kOutput, calls=%fused_computation.4 | convolution fusion | flops 2418016256 | bytes 4197378 | tf_op jit(solution)/shard_map/dot_general | solution.py:263
  (49 shorter events, 2.9 us)
Async XLA Ops:
  6.5 65.5 %copy-start.3 = (s32[64]{0:T(128)S(1)}, s32[64]{0:T(128)}, u32[]{:S(2)}) copy-start(s32[64]{0:T(128)} %param.12) | copy-start | bytes 772
  6.5 71.2 %copy-start.1 = (bf16[2,1,64,2048]{3,2,1,0:T(8,128)(2,1)S(1)}, bf16[2,1,64,2048]{3,2,1,0:T(8,128)(2,1)}, u32[]{:S(2)}) copy-start(bf16[2,1,64,2048]{3,2,1,0:T(8,128)(2,1)} %param.8) | copy-start | bytes 1572868
  6.5 217.6 %all-gather.3.cloned.1.call-start = ((), (), s32[]{:S(2)}) async-start(), calls=%async_computation.2 | async-start | bytes 9732096 | tf_op jit(solution)/shard_map/all_gather | solution.py:218
  13.0 44.4 %collective-permute-start = (bf16[9,64,128]{2,0,1:T(8,128)(2,1)S(1)}, bf16[9,64,128]{2,0,1:T(8,128)(2,1)S(1)}, u32[]{:S(2)}, u32[]{:S(2)}) collective-permute-start(bf16[9,64,128]{2,0,1:T(8,128)(2,1)S(1)} %pad_maximum_fusion.1), channel_id=1, source_target_pairs={{0,24},{1,25},{2,26},{3,27},{4,28},{5,29},{6,30},{7,31},{8,0},{9,1... | collective-permute-start | bytes 442376 | tf_op jit(solution)/shard_map/ppermute | solution.py:200
  35.8 25.6 %collective-permute-start.2 = (bf16[9,64,128]{2,0,1:T(8,128)(2,1)S(1)}, bf16[9,64,128]{2,0,1:T(8,128)(2,1)S(1)}, u32[]{:S(2)}, u32[]{:S(2)}) collective-permute-start(bf16[9,64,128]{2,0,1:T(8,128)(2,1)S(1)} %pad_maximum_fusion.2), channel_id=1, source_target_pairs={{0,7},{1,8},{2,9},{3,10},{4,11},{5,12},{6,13},{7,14},{8,15},{9,16}... | collective-permute-start | bytes 442376 | tf_op jit(solution)/shard_map/ppermute | solution.py:200
  57.4 7.9 %collective-permute-start.1 = (bf16[9,64,128]{2,0,1:T(8,128)(2,1)S(1)}, bf16[9,64,128]{2,0,1:T(8,128)(2,1)S(1)}, u32[]{:S(2)}, u32[]{:S(2)}) collective-permute-start(bf16[9,64,128]{2,0,1:T(8,128)(2,1)S(1)} %collective-permute-done), channel_id=1, source_target_pairs={{0,512},{1,577},{2,642},{3,707},{4,772},{5,837},{6,902},{7,967},{8... | collective-permute-start | bytes 442376 | tf_op jit(solution)/shard_map/ppermute | solution.py:207
  61.4 9.4 %collective-permute-start.3 = (bf16[9,64,128]{2,0,1:T(8,128)(2,1)S(1)}, bf16[9,64,128]{2,0,1:T(8,128)(2,1)S(1)}, u32[]{:S(2)}, u32[]{:S(2)}) collective-permute-start(bf16[9,64,128]{2,0,1:T(8,128)(2,1)S(1)} %collective-permute-done.2), channel_id=1, source_target_pairs={{0,576},{1,641},{2,706},{3,771},{4,836},{5,901},{6,966},{7,7},{8,7... | collective-permute-start | bytes 442376 | tf_op jit(solution)/shard_map/ppermute | solution.py:207
  70.9 16.7 %copy-start.2 = (f32[2048]{0:T(1024)S(1)}, f32[2048]{0:T(1024)}, u32[]{:S(2)}) copy-start(f32[2048]{0:T(1024)} %param.9) | copy-start | bytes 24580
  72.1 11.2 %collective-permute-start.6 = (f32[64,4]{0,1:T(4,128)S(1)}, f32[64,4]{0,1:T(4,128)S(1)}, u32[]{:S(2)}, u32[]{:S(2)}) collective-permute-start(f32[64,4]{0,1:T(4,128)S(1)} %get-tuple-element.33), channel_id=1, source_target_pairs={{0,64},{64,128},{128,192},{192,256},{256,320},{320,384},{384,448},... | collective-permute-start | bytes 3080 | tf_op jit(solution)/shard_map/ppermute | solution.py:19
  74.0 9.3 %collective-permute-start.7 = (f32[64,4]{0,1:T(4,128)S(1)}, f32[64,4]{0,1:T(4,128)S(1)}, u32[]{:S(2)}, u32[]{:S(2)}) collective-permute-start(f32[64,4]{0,1:T(4,128)S(1)} %get-tuple-element.32), channel_id=1, source_target_pairs={{64,0},{128,64},{192,128},{256,192},{320,256},{384,320},{448,384},... | collective-permute-start | bytes 3080 | tf_op jit(solution)/shard_map/ppermute | solution.py:19
  77.7 7.7 %collective-permute-start.4 = (bf16[64,2048]{1,0:T(8,128)(2,1)S(1)}, bf16[64,2048]{1,0:T(8,128)(2,1)S(1)}, u32[]{:S(2)}, u32[]{:S(2)}) collective-permute-start(bf16[64,2048]{1,0:T(8,128)(2,1)S(1)} %get-tuple-element.26), channel_id=1, source_target_pairs={{0,64},{64,128},{128,192},{192,256},{256,320},{320,384},{384,448},... | collective-permute-start | bytes 786440 | tf_op jit(solution)/shard_map/ppermute | solution.py:19
  80.9 6.3 %collective-permute-start.5 = (bf16[64,2048]{1,0:T(8,128)(2,1)S(1)}, bf16[64,2048]{1,0:T(8,128)(2,1)S(1)}, u32[]{:S(2)}, u32[]{:S(2)}) collective-permute-start(bf16[64,2048]{1,0:T(8,128)(2,1)S(1)} %get-tuple-element.27), channel_id=1, source_target_pairs={{64,0},{128,64},{192,128},{256,192},{320,256},{384,320},{448,384},... | collective-permute-start | bytes 786440 | tf_op jit(solution)/shard_map/ppermute | solution.py:19
  87.2 1.7 copy-start
  239.4 50.0 %all-to-all-start.1 = ((bf16[32,24,2048]{2,1,0:T(8,128)(2,1)}), bf16[32,24,2048]{2,1,0:T(8,128)(2,1)S(1)}, u32[]{:S(2)}, u32[]{:S(2)}) async-start(bf16[32,24,2048]{2,1,0:T(8,128)(2,1)} %bitcast.29), calls=%async_computation.1 | async-start | bytes 6291456 | tf_op jit(solution)/shard_map/all_to_all | solution.py:256
Sparse Core Ops, SparseCore 0:
  71.9 152.2 all-gather.2

commit v5 on v4

--- a/solution.py
+++ b/solution.py
@@ -30,10 +30,10 @@
     return jnp.sum(before * onehot, axis=-1)
 
 
-def expert_kernel(units, blocks, per_slot, place, rows_in, gathered, out, weights, hidden, sems):
+def expert_kernel(units, blocks, per_slot, stretch, place, rows_in, gathered, out, weights, hidden, sems):
     planes = gathered.shape[0]
     k_rows = gathered.shape[3]
-    total, width = rows_in.shape
+    width = rows_in.shape[2]
     per_unit = gathered.shape[1]
     sections = planes // units
 
@@ -48,69 +48,92 @@
                 sems.at[part, u, r],
             )
 
-    for part in range(3):
-        for u in range(units):
+    for u in range(units):
+        for part in range(2):
             for copy in copies(part, u):
                 copy.start()
+    for u in range(units):
+        for copy in copies(2, u):
+            copy.start()
 
     def arrive(part, u):
         for copy in copies(part, u):
             copy.wait()
 
-    for part in range(2):
-        for u in range(units):
-            arrive(part, u)
-    step = total // 3
-    for pair in range(0, units * blocks, 2):
-        columns = [(c // blocks, c % blocks) for c in (pair, pair + 1)]
-        at = [u * per_unit + b for u, b in columns]
-
-        def load(offset):
+    sources = rows_in.shape[0]
+    spare = stretch - per_slot
+    step = sources // 2
+    for u in range(units):
+        arrive(0, u)
+        arrive(1, u)
+
+        def load(*columns):
             return jnp.concatenate(
-                [weights[index + offset].reshape(width, LANES) for index in at], axis=1
+                [weights[u * per_unit + c].reshape(width, LANES) for c in columns], axis=1
             )
 
-        @pl.loop(0, total // step)
+        @pl.loop(0, sources // step)
         def _(i):
-            rows = pl.ds(pl.multiple_of(i * step, 16), step)
-            x = rows_in[rows, :]
-            gate = jnp.dot(x, load(0), preferred_element_type=jnp.float32)
-            up = jnp.dot(x, load(blocks), preferred_element_type=jnp.float32)
-            value = gate / (1.0 + jnp.exp(-gate)) * up
-            row = lax.broadcasted_iota(jnp.int32, value.shape, 0) + i * step
-            column = lax.broadcasted_iota(jnp.int32, value.shape, 1)
-            row_unit = row // per_slot % units
-            column_unit = jnp.where(column < LANES, columns[0][0], columns[1][0])
-            value = jnp.where(row_unit == column_unit, value, 0.0)
-            hidden[rows, pair * LANES : (pair + 2) * LANES] = value.astype(jnp.bfloat16)
+            at = pl.ds(i * step, step)
+            x = rows_in[at, u * (2 * per_slot - stretch) : u * (2 * per_slot - stretch) + stretch, :]
+            x = x.reshape(step * stretch, width)
+
+            def product(*columns):
+                return jnp.dot(x, load(*columns), preferred_element_type=jnp.float32)
+
+            row = lax.broadcasted_iota(jnp.int32, (step * stretch, LANES), 0)
+            row = lax.rem(row, stretch)
+            own = row < per_slot if u == 0 else row >= spare
+            gate_two = product(0, 1)
+            up_two = product(blocks, blocks + 1)
+            both = product(2, blocks + 2)
+            parts = [
+                (gate_two[:, :LANES], up_two[:, :LANES]),
+                (gate_two[:, LANES:], up_two[:, LANES:]),
+                (both[:, :LANES], both[:, LANES:]),
+            ]
+            out_rows = pl.ds(pl.multiple_of(i * (step * stretch), step * stretch), step * stretch)
+            for b, (gate, up) in enumerate(parts):
+                value = gate / (1.0 + jnp.exp(-gate)) * up
+                value = jnp.where(own, value, 0.0).astype(jnp.bfloat16)
+                hidden[u, out_rows, b * LANES : (b + 1) * LANES] = value
 
     for u in range(units):
         arrive(2, u)
+    edge = 2 * per_slot - stretch
     for first in range(0, sections, 2):
 
-        def down(b):
+        def down(u, b):
             parts = [
-                weights[u * per_unit + 2 * blocks + i, a, b]
-                for u in range(units)
-                for a in range(2)
-                for i in range(blocks)
+                weights[u * per_unit + 2 * blocks + i, a, b] for a in range(2) for i in range(blocks)
             ]
             return jnp.concatenate(parts, axis=0)
 
-        w = jnp.concatenate([down(first), down(first + 1)], axis=1)
-        out[:, first * LANES : (first + 2) * LANES] = jnp.dot(
-            hidden[...], w, preferred_element_type=jnp.float32
-        ).astype(jnp.bfloat16)
+        y = []
+        for u in range(units):
+            w = jnp.concatenate([down(u, first), down(u, first + 1)], axis=1)
+            y.append(
+                jnp.dot(hidden[u], w, preferred_element_type=jnp.float32).reshape(
+                    sources, stretch, 2 * LANES
+                )
+            )
+        joined = jnp.concatenate(
+            [y[0][:, :edge], y[0][:, edge:] + y[1][:, : stretch - edge], y[1][:, stretch - edge :]],
+            axis=1,
+        )
+        out[:, :, first * LANES : (first + 2) * LANES] = joined.astype(jnp.bfloat16)
 
 
 def run_experts(received, gathered, place, units, blocks, per_slot, ff):
-    total, width = received.shape
+    sources, per_host, width = received.shape
+    total = sources * per_host
+    stretch = -(-per_slot // 8) * 8
     vmem = pl.BlockSpec(memory_space=pltpu.VMEM)
     planes, per_unit, pieces, k_rows, lanes = gathered.shape
     shape = (units * per_unit, pieces, planes // units, k_rows, lanes)
     return pl.pallas_call(
-        functools.partial(expert_kernel, units, blocks, per_slot),
-        out_shape=jax.ShapeDtypeStruct((total, width), jnp.bfloat16),
+        functools.partial(expert_kernel, units, blocks, per_slot, stretch),
+        out_shape=jax.ShapeDtypeStruct(received.shape, jnp.bfloat16),
         in_specs=[
             pl.BlockSpec(memory_space=pltpu.SMEM),
             vmem,
@@ -119,7 +142,7 @@
         out_specs=vmem,
         scratch_shapes=[
             pltpu.VMEM(shape, jnp.bfloat16),
-            pltpu.VMEM((total, ff), jnp.bfloat16),
+            pltpu.VMEM((units, sources * stretch, ff // units), jnp.bfloat16),
             pltpu.SemaphoreType.DMA((3, units, planes // units)),
         ],
         cost_estimate=pl.CostEstimate(
@@ -148,12 +171,10 @@
     top = expert_ids.shape[3]
     micros = tokens.shape[0]
 
-    expert_range = jnp.arange(experts, dtype=jnp.int32)
-    owner = (placement[:, None] == expert_range[None, :]).astype(jnp.int32)
-    slot_rank = exclusive_rank(owner)
     slot_range = jnp.arange(slots, dtype=jnp.int32)
-    mine = slot_range == side * planes + plane
-    half = jnp.sum(jnp.where(mine, slot_rank, 0)) % 2
+    mine = side * planes + plane
+    my_expert = jnp.sum(jnp.where(slot_range == mine, placement, 0))
+    half = jnp.sum(((placement == my_expert) & (slot_range < mine)).astype(jnp.int32)) % 2
 
     k_rows = width // planes
     f_rows = half_ff // units
@@ -164,14 +185,14 @@
             part = lax.dynamic_slice(
                 w[0], (number * k_rows, half * half_ff), (k_rows, half_ff)
             )
-            return part.reshape(k_rows, blocks, LANES).transpose(1, 0, 2)
+            return [part[:, b * LANES : (b + 1) * LANES] for b in range(blocks)]
 
         down = lax.dynamic_slice(
             w_down[0],
             (half * half_ff + number // sections * f_rows, number % sections * LANES),
             (f_rows, LANES),
-        ).reshape(f_rows // k_rows, k_rows, LANES)
-        return jnp.concatenate([columns(w_gate), columns(w_up), down], axis=0)
+        )
+        return jnp.concatenate([*columns(w_gate), *columns(w_up), down], axis=0)
 
     quarter = sections // 4
 
@@ -205,10 +226,16 @@
             for m in range(planes)
         ]
         arrived[i] = lax.ppermute(arrived[i], ("section", "plane"), moves)
-    share = jnp.stack(arrived, axis=1)
+    share = jnp.stack([x.reshape(-1, k_rows, LANES) for x in arrived], axis=1)
+    share = share.reshape(-1, LANES)
 
     routing = jnp.concatenate([expert_ids[:, 0].astype(jnp.float32), route_scores[:, 0]], axis=-1)
-    share, tokens, routing = lax.optimization_barrier((share, tokens, routing))
+    share, tokens, routing, placement = lax.optimization_barrier(
+        (share, tokens, routing, placement)
+    )
+    expert_range = jnp.arange(experts, dtype=jnp.int32)
+    owner = (placement[:, None] == expert_range[None, :]).astype(jnp.int32)
+    slot_rank = exclusive_rank(owner)
     ways = (1, -1)
     tokens = jnp.stack([passed_along(tokens[m, 0], "section", ways[m]) for m in range(micros)])
     routing = jnp.stack([passed_along(routing[m], "section", ways[m]) for m in range(micros)])
@@ -216,6 +243,7 @@
     expert_ids = routing[:, :, :top].astype(jnp.int32)
     scores = routing[:, :, top:]
     gathered = lax.all_gather(share, "plane", axis=0)
+    gathered = gathered.reshape(planes, -1, 2, k_rows, LANES)
     per_slot = micros * MOST
     per_host = units * per_slot
     slot_side = slot_range // planes
@@ -253,17 +281,16 @@
 
     def exchange(x):
         x = x.reshape(hosts, per_host, width)
-        x = lax.all_to_all(x, ("section", "side"), split_axis=0, concat_axis=0, tiled=True)
-        return x.reshape(total, width)
+        return lax.all_to_all(x, ("section", "side"), split_axis=0, concat_axis=0, tiled=True)
 
     received = exchange(send)
     place = jnp.full((1,), section, jnp.int32)
     partial = run_experts(received, gathered, place, units, blocks, per_slot, ff)
-    returned = exchange(partial)
+    returned = exchange(partial).reshape(total, width)
     moe = jnp.dot(
         mixing,
         returned.astype(jnp.float32),
-        precision=lax.Precision.HIGHEST,
+        precision=lax.Precision.HIGH,
         preferred_element_type=jnp.float32,
     )
     mixed = tokens.astype(jnp.float32) + moe.reshape(micros, tok_rows, width)

time: 300 us -> 286 us (0.953)
  waiting for transfers between devices: 151 us -> 140 us
  Pallas kernels: 15.3 us -> 10.9 us
    ppermute x2, waiting for transfers between devices: 16.3 us -> 10.7 us  [body(): arrived.append(lax.ppermute(piece(number), ('section', 'plane'), moves))]
    pallas_call x1, Pallas kernels: 15.3 us -> 10.9 us  [run_experts(): pl.pallas_call(functools.partial(expert_kernel, units, blocks, per_slot,...]
    reduce_sum x0 -> x2, other arithmetic: none -> 3.38 us  [the longest x1 2.02 us: body(): jnp.sum(((placement == my_expert) & (slot_range < mine)).astype(jnp.int32))]
  transfers between devices with their start and end apart: 10 -> 10, of which waited for: 7 -> 6; matrix products, arithmetic and copies ran while one was open for 2% -> 3% of each run, Pallas kernels for 0% -> 0%
where the time goes in v5:
time: 286 us; the launch traced here: 285 us
  waiting for transfers between devices  140 us (49%)
  starting transfers between devices  50.7 us (18%)
  blocking collectives  50.6 us (18%)
  between operations  15.9 us (6%)
  Pallas kernels  10.9 us (4%)
  other arithmetic  7.85 us (3%)
  local copies, waits for them, and re-layouts  4.52 us (2%)
  matrix products  4.11 us (1%)
    all_gather x1, waiting for transfers between devices, body(): gathered = lax.all_gather(share, 'plane', axis=0)  82.2 us
    all_to_all x1, blocking collectives, exchange(): lax.all_to_all(x, ('section', 'side'), split_axis=0, concat_axis=0, tiled...  50.6 us
    all_to_all x1, waiting for transfers between devices, exchange(): lax.all_to_all(x, ('section', 'side'), split_axis=0, concat_axis=0, tiled...  42.6 us
    ppermute x2, starting transfers between devices, body(): arrived.append(lax.ppermute(piece(number), ('section', 'plane'), moves))  27.8 us
    ppermute x4, starting transfers between devices, passed_along(): return lax.ppermute(x, axis, pairs)  11.2 us
    pallas_call x1, Pallas kernels, run_experts(): pl.pallas_call(functools.partial(expert_kernel, units, blocks, per_slot,...  10.9 us
    ppermute x2, waiting for transfers between devices, body(): arrived.append(lax.ppermute(piece(number), ('section', 'plane'), moves))  10.7 us
    all_to_all x1, starting transfers between devices, exchange(): lax.all_to_all(x, ('section', 'side'), split_axis=0, concat_axis=0, tiled...  7.57 us
  transfers between devices with their start and end apart: 10, of which 6 were waited for; matrix products, arithmetic and copies ran while one was open for 3% of the time, Pallas kernels for 0%

profile of v5, /device:TPU:2, one launch (start us, length us, event | category | flops | bytes accessed | tf_op | source)
XLA Modules:
  0.0 285.1 jit_solution(13946706803535826401)
XLA Ops:
  6.5 1.4 fusion.31
  7.9 2.0 fusion.33
  12.1 0.9 dynamic-slice_bitcast_fusion.2
  13.2 0.8 bitcast_dynamic-update-slice_fusion.1
  14.1 22.6 %collective-permute-start = (bf16[576,128]{1,0:T(8,128)(2,1)S(1)}, bf16[576,128]{1,0:T(8,128)(2,1)S(1)}, u32[]{:S(2)}, u32[]{:S(2)}) collective-permute-start(bf16[576,128]{1,0:T(8,128)(2,1)S(1)} %get-tuple-element.22), channel_id=1, source_target_pairs={{0,24},{1,25},{2,26},{3,27},{4,28},{5,29},{6,30},{7,31},{8,0},{9,1... | collective-permute-start | bytes 442376 | tf_op jit(solution)/shard_map/ppermute | solution.py:221
  36.6 5.2 %collective-permute-start.2 = (bf16[576,128]{1,0:T(8,128)(2,1)S(1)}, bf16[576,128]{1,0:T(8,128)(2,1)S(1)}, u32[]{:S(2)}, u32[]{:S(2)}) collective-permute-start(bf16[576,128]{1,0:T(8,128)(2,1)S(1)} %get-tuple-element.23), channel_id=1, source_target_pairs={{0,7},{1,8},{2,9},{3,10},{4,11},{5,12},{6,13},{7,14},{8,15},{9,16}... | collective-permute-start | bytes 442376 | tf_op jit(solution)/shard_map/ppermute | solution.py:221
  41.8 7.0 %collective-permute-done = bf16[576,128]{1,0:T(8,128)(2,1)S(1)} collective-permute-done((bf16[576,128]{1,0:T(8,128)(2,1)S(1)}, bf16[576,128]{1,0:T(8,128)(2,1)S(1)}, u32[]{:S(2)}, u32[]{:S(2)}) %collective-permute-start) | collective-permute-done | bytes 147488 | tf_op jit(solution)/shard_map/ppermute | solution.py:221
  48.8 2.3 collective-permute-start.1
  51.1 3.7 %collective-permute-done.2 = bf16[576,128]{1,0:T(8,128)(2,1)S(1)} collective-permute-done((bf16[576,128]{1,0:T(8,128)(2,1)S(1)}, bf16[576,128]{1,0:T(8,128)(2,1)S(1)}, u32[]{:S(2)}, u32[]{:S(2)}) %collective-permute-start.2) | collective-permute-done | bytes 147488 | tf_op jit(solution)/shard_map/ppermute | solution.py:221
  54.8 1.9 collective-permute-start.3
  56.7 0.7 fusion.27
  57.4 0.7 pad_maximum_fusion.1
  58.1 3.2 %collective-permute-done.3 = bf16[576,128]{1,0:T(8,128)(2,1)S(1)} collective-permute-done((bf16[576,128]{1,0:T(8,128)(2,1)S(1)}, bf16[576,128]{1,0:T(8,128)(2,1)S(1)}, u32[]{:S(2)}, u32[]{:S(2)}) %collective-permute-start.3) | collective-permute-done | bytes 147488 | tf_op jit(solution)/shard_map/ppermute | solution.py:228
  61.3 0.7 pad_maximum_fusion
  62.3 1.9 collective-permute-start.6
  64.2 3.8 %collective-permute-start.7 = (f32[64,4]{0,1:T(4,128)S(1)}, f32[64,4]{0,1:T(4,128)S(1)}, u32[]{:S(2)}, u32[]{:S(2)}) collective-permute-start(f32[64,4]{0,1:T(4,128)S(1)} %get-tuple-element.34), channel_id=1, source_target_pairs={{64,0},{128,64},{192,128},{256,192},{320,256},{384,320},{448,384},... | collective-permute-start | bytes 3080 | tf_op jit(solution)/shard_map/ppermute | solution.py:19
  68.0 0.7 fusion.24
  68.8 1.1 slice_bitcast_fusion.1
  69.9 1.9 collective-permute-start.4
  71.8 3.6 %collective-permute-start.5 = (bf16[64,2048]{1,0:T(8,128)(2,1)S(1)}, bf16[64,2048]{1,0:T(8,128)(2,1)S(1)}, u32[]{:S(2)}, u32[]{:S(2)}) collective-permute-start(bf16[64,2048]{1,0:T(8,128)(2,1)S(1)} %get-tuple-element.29), channel_id=1, source_target_pairs={{64,0},{128,64},{192,128},{256,192},{320,256},{384,320},{448,384},... | collective-permute-start | bytes 786440 | tf_op jit(solution)/shard_map/ppermute | solution.py:19
  76.2 0.2 reduce_window_sum.23
  76.4 0.3 select_reduce_fusion.2
  77.4 0.2 slice_reduce_fusion.1
  77.6 1.7 collective-permute-done.5
  79.3 0.2 multiply_reduce_fusion
  79.8 1.2 convolution_convert_fusion
  81.0 50.6 %all_to_all.10.rows_in = bf16[32,24,2048]{2,1,0:T(8,128)(2,1)S(1)} all-to-all(bf16[32,24,2048]{2,1,0:T(8,128)(2,1)S(1)} %bitcast.59), channel_id=1, replica_groups=mesh['section'=16,'side'=2,'plane'=32] {'section','side'}, dimensions={0} | all-to-all | bytes 6291456 | tf_op jit(solution)/shard_map/all_to_all | solution.py:284
  131.6 82.2 %all-gather.3.cloned.1.call-done = bf16[36864,128]{1,0:T(8,128)(2,1)} async-done(((bf16[1152,128]{1,0:T(8,128)(2,1)}), bf16[36864,128]{1,0:T(8,128)(2,1)}) %all-gather.3.cloned.1.call-update) | async-done | bytes 9437200 | tf_op jit(solution)/shard_map/all_gather | solution.py:245
  213.9 10.9 %shard_map.82 = bf16[32,24,2048]{2,1,0:T(8,128)(2,1)} custom-call(s32[1]{0:T(128)} %bitcast.25.place, bf16[32,24,2048]{2,1,0:T(8,128)(2,1)S(1)} %all_to_all.10.rows_in, bf16[32,9,2,64,128]{4,3,2,1,0:T(8,128)(2,1)} %bitcast.77), custom_call_target="tpu_custom_call" | custom-call | flops 7247757312 | bytes 15728640 | tf_op jit(solution)/shard_map/pallas_call | solution.py:134
  224.8 7.6 %all-to-all-start.1 = ((bf16[32,24,2048]{2,1,0:T(8,128)(2,1)}), bf16[32,24,2048]{2,1,0:T(8,128)(2,1)S(1)}, u32[]{:S(2)}, u32[]{:S(2)}) async-start(bf16[32,24,2048]{2,1,0:T(8,128)(2,1)} %shard_map.82), calls=%async_computation.1 | async-start | bytes 6291456 | tf_op jit(solution)/shard_map/all_to_all | solution.py:284
  232.7 42.6 %all-to-all-done.1 = bf16[32,24,2048]{2,1,0:T(8,128)(2,1)S(1)} async-done(((bf16[32,24,2048]{2,1,0:T(8,128)(2,1)}), bf16[32,24,2048]{2,1,0:T(8,128)(2,1)S(1)}, u32[]{:S(2)}, u32[]{:S(2)}) %all-to-all-start.1) | async-done | bytes 3145760 | tf_op jit(solution)/shard_map/all_to_all | solution.py:284
  275.3 3.0 %fusion.2 = bf16[2,1,64,2048]{3,2,1,0:T(8,128)(2,1)} fusion(bf16[768,2048,1]{1,0,2:T(8,128)(2,1)S(1)} %bitcast.60, pred[2]{0:T(512)(128)(4,1)S(1)} %pad_add_fusion, s32[2,64]{1,0:T(2,128)S(1)} %eq.256, s32[2,64]{1,0:T(2,128)S(1)} %eq.252, f32[2,64]{1,0:T(2,128)S(1)} %bitcast.76, s32[2,64]{1,0:T(2,128)S(1)} %eq.247, f32[2,64]{1,0:T(2,128)S(1)} %bitcast.75, ...), kind=kOutput, calls=%fused_computation.4 | convolution fusion | flops 1210056704 | bytes 4197378 | tf_op jit(solution)/shard_map/dot_general | solution.py:290
  (52 shorter events, 2.5 us)
Async XLA Ops:
  6.5 68.9 %copy-start.2 = (s32[64]{0:T(128)S(1)}, s32[64]{0:T(128)}, u32[]{:S(2)}) copy-start(s32[64]{0:T(128)} %param.12) | copy-start | bytes 772
  6.5 207.3 %all-gather.3.cloned.1.call-start = ((), (), s32[]{:S(2)}) async-start(), calls=%async_computation.2 | async-start | bytes 9732096 | tf_op jit(solution)/shard_map/all_gather | solution.py:245
  13.0 66.6 %copy-start.1 = (f32[2048]{0:T(1024)S(1)}, f32[2048]{0:T(1024)}, u32[]{:S(2)}) copy-start(f32[2048]{0:T(1024)} %param.9) | copy-start | bytes 24580
  14.1 34.8 %collective-permute-start = (bf16[576,128]{1,0:T(8,128)(2,1)S(1)}, bf16[576,128]{1,0:T(8,128)(2,1)S(1)}, u32[]{:S(2)}, u32[]{:S(2)}) collective-permute-start(bf16[576,128]{1,0:T(8,128)(2,1)S(1)} %get-tuple-element.22), channel_id=1, source_target_pairs={{0,24},{1,25},{2,26},{3,27},{4,28},{5,29},{6,30},{7,31},{8,0},{9,1... | collective-permute-start | bytes 442376 | tf_op jit(solution)/shard_map/ppermute | solution.py:221
  36.6 18.2 %collective-permute-start.2 = (bf16[576,128]{1,0:T(8,128)(2,1)S(1)}, bf16[576,128]{1,0:T(8,128)(2,1)S(1)}, u32[]{:S(2)}, u32[]{:S(2)}) collective-permute-start(bf16[576,128]{1,0:T(8,128)(2,1)S(1)} %get-tuple-element.23), channel_id=1, source_target_pairs={{0,7},{1,8},{2,9},{3,10},{4,11},{5,12},{6,13},{7,14},{8,15},{9,16}... | collective-permute-start | bytes 442376 | tf_op jit(solution)/shard_map/ppermute | solution.py:221
  48.8 9.3 %collective-permute-start.1 = (bf16[576,128]{1,0:T(8,128)(2,1)S(1)}, bf16[576,128]{1,0:T(8,128)(2,1)S(1)}, u32[]{:S(2)}, u32[]{:S(2)}) collective-permute-start(bf16[576,128]{1,0:T(8,128)(2,1)S(1)} %collective-permute-done), channel_id=1, source_target_pairs={{0,512},{1,577},{2,642},{3,707},{4,772},{5,837},{6,902},{7,967},{8... | collective-permute-start | bytes 442376 | tf_op jit(solution)/shard_map/ppermute | solution.py:228
  54.8 6.5 %collective-permute-start.3 = (bf16[576,128]{1,0:T(8,128)(2,1)S(1)}, bf16[576,128]{1,0:T(8,128)(2,1)S(1)}, u32[]{:S(2)}, u32[]{:S(2)}) collective-permute-start(bf16[576,128]{1,0:T(8,128)(2,1)S(1)} %collective-permute-done.2), channel_id=1, source_target_pairs={{0,576},{1,641},{2,706},{3,771},{4,836},{5,901},{6,966},{7,7},{8,7... | collective-permute-start | bytes 442376 | tf_op jit(solution)/shard_map/ppermute | solution.py:228
  62.3 13.5 %collective-permute-start.6 = (f32[64,4]{0,1:T(4,128)S(1)}, f32[64,4]{0,1:T(4,128)S(1)}, u32[]{:S(2)}, u32[]{:S(2)}) collective-permute-start(f32[64,4]{0,1:T(4,128)S(1)} %get-tuple-element.35), channel_id=1, source_target_pairs={{0,64},{64,128},{128,192},{192,256},{256,320},{320,384},{384,448},... | collective-permute-start | bytes 3080 | tf_op jit(solution)/shard_map/ppermute | solution.py:19
  64.2 11.6 %collective-permute-start.7 = (f32[64,4]{0,1:T(4,128)S(1)}, f32[64,4]{0,1:T(4,128)S(1)}, u32[]{:S(2)}, u32[]{:S(2)}) collective-permute-start(f32[64,4]{0,1:T(4,128)S(1)} %get-tuple-element.34), channel_id=1, source_target_pairs={{64,0},{128,64},{192,128},{256,192},{320,256},{384,320},{448,384},... | collective-permute-start | bytes 3080 | tf_op jit(solution)/shard_map/ppermute | solution.py:19
  69.9 7.7 %collective-permute-start.4 = (bf16[64,2048]{1,0:T(8,128)(2,1)S(1)}, bf16[64,2048]{1,0:T(8,128)(2,1)S(1)}, u32[]{:S(2)}, u32[]{:S(2)}) collective-permute-start(bf16[64,2048]{1,0:T(8,128)(2,1)S(1)} %get-tuple-element.28), channel_id=1, source_target_pairs={{0,64},{64,128},{128,192},{192,256},{256,320},{320,384},{384,448},... | collective-permute-start | bytes 786440 | tf_op jit(solution)/shard_map/ppermute | solution.py:19
  71.8 7.5 %collective-permute-start.5 = (bf16[64,2048]{1,0:T(8,128)(2,1)S(1)}, bf16[64,2048]{1,0:T(8,128)(2,1)S(1)}, u32[]{:S(2)}, u32[]{:S(2)}) collective-permute-start(bf16[64,2048]{1,0:T(8,128)(2,1)S(1)} %get-tuple-element.29), channel_id=1, source_target_pairs={{64,0},{128,64},{192,128},{256,192},{320,256},{384,320},{448,384},... | collective-permute-start | bytes 786440 | tf_op jit(solution)/shard_map/ppermute | solution.py:19
  79.3 1.7 copy-start
  224.8 50.5 %all-to-all-start.1 = ((bf16[32,24,2048]{2,1,0:T(8,128)(2,1)}), bf16[32,24,2048]{2,1,0:T(8,128)(2,1)S(1)}, u32[]{:S(2)}, u32[]{:S(2)}) async-start(bf16[32,24,2048]{2,1,0:T(8,128)(2,1)} %shard_map.82), calls=%async_computation.1 | async-start | bytes 6291456 | tf_op jit(solution)/shard_map/all_to_all | solution.py:284
Sparse Core Ops, SparseCore 0:
  62.1 151.6 all-gather.2

commit v6 on v5

--- a/solution.py
+++ b/solution.py
@@ -154,6 +154,68 @@
     )(place, received, gathered)
 
 
+def piece_kernel(sections, planes, k_rows, half_ff, placement, w_gate, w_up, w_down, *rest):
+    *outs, sems = rest
+    section = lax.axis_index("section")
+    plane = lax.axis_index("plane")
+    mine = lax.axis_index("side") * planes + plane
+    blocks = half_ff // LANES
+    f_rows = half_ff // 2
+    my_expert = placement[mine]
+
+    def count(s, total):
+        return total + jnp.where((placement[s] == my_expert) & (s < mine), 1, 0)
+
+    half = lax.rem(lax.fori_loop(0, placement.shape[0], count, 0, unroll=8), 2)
+    quarter = sections // 4
+    step = lax.rem(lax.div(section, 2), quarter)
+    even = lax.rem(section, 2) == 0
+    back = jnp.where(even, step - sections // 2, -1 - step)
+    ahead = jnp.where(even, sections // 2 - 1 - step, step)
+    copies = []
+    for i, out in enumerate(outs):
+        distance = jnp.where((lax.div(section, 2) < quarter) == (i == 0), back, ahead)
+        place = lax.rem(plane + distance + planes, sections)
+        rows = pl.ds(pl.multiple_of((i * sections + place) * k_rows, k_rows), k_rows)
+        parts = []
+        for w in (w_gate, w_up):
+            for b in range(blocks):
+                columns = pl.ds(pl.multiple_of(half * half_ff + b * LANES, LANES), LANES)
+                parts.append((w.at[0, rows, columns], k_rows))
+        rows = pl.ds(pl.multiple_of(half * half_ff + i * f_rows, k_rows), f_rows)
+        parts.append((w_down.at[0, rows, pl.ds(pl.multiple_of(place * LANES, LANES), LANES)], f_rows))
+        first = 0
+        for part, length in parts:
+            copies.append(
+                pltpu.make_async_copy(part, out.at[pl.ds(first, length)], sems.at[len(copies)])
+            )
+            first += length
+    for copy in copies:
+        copy.start()
+    for copy in copies:
+        copy.wait()
+
+
+def cut_pieces(placement, w_gate, w_up, w_down, sections, planes):
+    width, ff = w_gate.shape[1:]
+    half_ff = ff // 2
+    k_rows = width // planes
+    lines = 2 * (half_ff // LANES) * k_rows + half_ff // 2
+    shape = jax.ShapeDtypeStruct((lines, LANES), w_gate.dtype)
+    vmem = pl.BlockSpec(memory_space=pltpu.VMEM)
+    hbm = pl.BlockSpec(memory_space=pl.ANY)
+    return pl.pallas_call(
+        functools.partial(piece_kernel, sections, planes, k_rows, half_ff),
+        out_shape=(shape, shape),
+        in_specs=[pl.BlockSpec(memory_space=pltpu.SMEM), hbm, hbm, hbm],
+        out_specs=(vmem, vmem),
+        scratch_shapes=[pltpu.SemaphoreType.DMA((2 * (2 * (half_ff // LANES) + 1),))],
+        cost_estimate=pl.CostEstimate(
+            flops=0, bytes_accessed=8 * lines * LANES, transcendentals=0
+        ),
+    )(placement, w_gate, w_up, w_down)
+
+
 def body(tokens, norm_gain, expert_ids, route_scores, placement, w_gate, w_up, w_down):
     sections = lax.axis_size("section")
     sides = lax.axis_size("side")
@@ -171,28 +233,10 @@
     top = expert_ids.shape[3]
     micros = tokens.shape[0]
 
+    expert_range = jnp.arange(experts, dtype=jnp.int32)
     slot_range = jnp.arange(slots, dtype=jnp.int32)
-    mine = side * planes + plane
-    my_expert = jnp.sum(jnp.where(slot_range == mine, placement, 0))
-    half = jnp.sum(((placement == my_expert) & (slot_range < mine)).astype(jnp.int32)) % 2
-
     k_rows = width // planes
-    f_rows = half_ff // units
     blocks = half_ff // LANES
-
-    def piece(number):
-        def columns(w):
-            part = lax.dynamic_slice(
-                w[0], (number * k_rows, half * half_ff), (k_rows, half_ff)
-            )
-            return [part[:, b * LANES : (b + 1) * LANES] for b in range(blocks)]
-
-        down = lax.dynamic_slice(
-            w_down[0],
-            (half * half_ff + number // sections * f_rows, number % sections * LANES),
-            (f_rows, LANES),
-        )
-        return jnp.concatenate([*columns(w_gate), *columns(w_up), down], axis=0)
 
     quarter = sections // 4
 
@@ -202,23 +246,15 @@
         ahead = (sections // 2 - 1 - step) if q % 2 == 0 else step
         return back if (q // 2 < quarter) == (i == 0) else ahead
 
-    def my_distance(i):
-        step = section // 2 % quarter
-        even = section % 2 == 0
-        back = jnp.where(even, step - sections // 2, -1 - step)
-        ahead = jnp.where(even, sections // 2 - 1 - step, step)
-        return jnp.where((section // 2 < quarter) == (i == 0), back, ahead)
-
+    pieces = cut_pieces(placement, w_gate, w_up, w_down, sections, planes)
     arrived = []
     for i in range(2):
-        target = (plane + my_distance(i)) % planes
-        number = i * sections + target % sections
         moves = [
             (q * planes + j, q * planes + (j + distance(q, i)) % planes)
             for q in range(sections)
             for j in range(planes)
         ]
-        arrived.append(lax.ppermute(piece(number), ("section", "plane"), moves))
+        arrived.append(lax.ppermute(pieces[i], ("section", "plane"), moves))
     for i in range(2):
         moves = [
             (q * planes + m, (m - distance(q, i)) % sections * planes + m)
@@ -233,7 +269,6 @@
     share, tokens, routing, placement = lax.optimization_barrier(
         (share, tokens, routing, placement)
     )
-    expert_range = jnp.arange(experts, dtype=jnp.int32)
     owner = (placement[:, None] == expert_range[None, :]).astype(jnp.int32)
     slot_rank = exclusive_rank(owner)
     ways = (1, -1)

time: 286 us -> 281 us (0.983)
  waiting for transfers between devices: 140 us -> 149 us
  other arithmetic: 7.85 us -> 1.74 us
  blocking collectives: 50.6 us -> 46.6 us
    all_gather x1, waiting for transfers between devices: 82.2 us -> 87.1 us  [body(): gathered = lax.all_gather(share, 'plane', axis=0)]
    all_to_all x1, blocking collectives: 50.6 us -> 46.6 us  [exchange(): lax.all_to_all(x, ('section', 'side'), split_axis=0, concat_axis=0, tiled...]
    reduce_sum x2 -> x0, other arithmetic: 3.38 us -> none  [the longest x1 2.02 us: body(): jnp.sum(((placement == my_expert) & (slot_range < mine)).astype(jnp.int32))]
  transfers between devices with their start and end apart: 10 -> 10, of which waited for: 6 -> 6; matrix products, arithmetic and copies ran while one was open for 3% -> 2% of each run, Pallas kernels for 0% -> 0%
where the time goes in v6:
time: 281 us
  waiting for transfers between devices  149 us (53%)
  starting transfers between devices  49.8 us (18%)
  blocking collectives  46.6 us (17%)
  Pallas kernels  13.7 us (5%)
  between operations  13.7 us (5%)
  matrix products  4.07 us (1%)
    all_gather x1, waiting for transfers between devices, body(): gathered = lax.all_gather(share, 'plane', axis=0)  87.1 us
    all_to_all x1, blocking collectives, exchange(): lax.all_to_all(x, ('section', 'side'), split_axis=0, concat_axis=0, tiled...  46.6 us
    all_to_all x1, waiting for transfers between devices, exchange(): lax.all_to_all(x, ('section', 'side'), split_axis=0, concat_axis=0, tiled...  42.6 us
    ppermute x2, starting transfers between devices, body(): arrived.append(lax.ppermute(pieces[i], ('section', 'plane'), moves))  27.8 us
    ppermute x2, waiting for transfers between devices, body(): arrived.append(lax.ppermute(pieces[i], ('section', 'plane'), moves))  10.9 us
    pallas_call x1, Pallas kernels, run_experts(): pl.pallas_call(functools.partial(expert_kernel, units, blocks, per_slot,...  10.9 us
    ppermute x4, starting transfers between devices, passed_along(): return lax.ppermute(x, axis, pairs)  10.2 us
    all_to_all x1, starting transfers between devices, exchange(): lax.all_to_all(x, ('section', 'side'), split_axis=0, concat_axis=0, tiled...  7.65 us
  transfers between devices with their start and end apart: 10, of which 6 were waited for; matrix products, arithmetic and copies ran while one was open for 2% of the time, Pallas kernels for 0%

profile of v6, /device:TPU:2, one launch (start us, length us, event | category | flops | bytes accessed | tf_op | source)
XLA Modules:
  0.0 280.6 jit_solution(16657471583085111682)
XLA Ops:
  6.6 2.8 shard_map.82
  9.4 22.6 %collective-permute-start = (bf16[576,128]{1,0:T(8,128)(2,1)}, bf16[576,128]{1,0:T(8,128)(2,1)S(1)}, u32[]{:S(2)}, u32[]{:S(2)}) collective-permute-start(bf16[576,128]{1,0:T(8,128)(2,1)} %get-tuple-element.11), channel_id=1, source_target_pairs={{0,24},{1,25},{2,26},{3,27},{4,28},{5,29},{6,30},{7,31},{8,0},{9,1... | collective-permute-start | bytes 442376 | tf_op jit(solution)/shard_map/ppermute | solution.py:257
  32.0 5.2 %collective-permute-start.2 = (bf16[576,128]{1,0:T(8,128)(2,1)}, bf16[576,128]{1,0:T(8,128)(2,1)S(1)}, u32[]{:S(2)}, u32[]{:S(2)}) collective-permute-start(bf16[576,128]{1,0:T(8,128)(2,1)} %get-tuple-element.12), channel_id=1, source_target_pairs={{0,7},{1,8},{2,9},{3,10},{4,11},{5,12},{6,13},{7,14},{8,15},{9,16}... | collective-permute-start | bytes 442376 | tf_op jit(solution)/shard_map/ppermute | solution.py:257
  37.2 7.3 %collective-permute-done = bf16[576,128]{1,0:T(8,128)(2,1)S(1)} collective-permute-done((bf16[576,128]{1,0:T(8,128)(2,1)}, bf16[576,128]{1,0:T(8,128)(2,1)S(1)}, u32[]{:S(2)}, u32[]{:S(2)}) %collective-permute-start) | collective-permute-done | bytes 147488 | tf_op jit(solution)/shard_map/ppermute | solution.py:257
  44.5 2.3 collective-permute-start.1
  46.8 3.6 %collective-permute-done.2 = bf16[576,128]{1,0:T(8,128)(2,1)S(1)} collective-permute-done((bf16[576,128]{1,0:T(8,128)(2,1)}, bf16[576,128]{1,0:T(8,128)(2,1)S(1)}, u32[]{:S(2)}, u32[]{:S(2)}) %collective-permute-start.2) | collective-permute-done | bytes 147488 | tf_op jit(solution)/shard_map/ppermute | solution.py:257
  50.3 1.9 collective-permute-start.3
  52.3 4.5 %collective-permute-done.3 = bf16[576,128]{1,0:T(8,128)(2,1)S(1)} collective-permute-done((bf16[576,128]{1,0:T(8,128)(2,1)S(1)}, bf16[576,128]{1,0:T(8,128)(2,1)S(1)}, u32[]{:S(2)}, u32[]{:S(2)}) %collective-permute-start.3) | collective-permute-done | bytes 147488 | tf_op jit(solution)/shard_map/ppermute | solution.py:264
  56.8 0.7 copy.16
  58.0 1.9 collective-permute-start.6
  59.9 3.6 %collective-permute-start.7 = (f32[64,4]{0,1:T(4,128)S(1)}, f32[64,4]{0,1:T(4,128)S(1)}, u32[]{:S(2)}, u32[]{:S(2)}) collective-permute-start(f32[64,4]{0,1:T(4,128)S(1)} %get-tuple-element.32), channel_id=1, source_target_pairs={{64,0},{128,64},{192,128},{256,192},{320,256},{384,320},{448,384},... | collective-permute-start | bytes 3080 | tf_op jit(solution)/shard_map/ppermute | solution.py:19
  63.7 2.7 collective-permute-start.5
  66.3 1.9 collective-permute-start.4
  68.3 0.2 select_reduce_fusion.5
  68.5 0.1 select_reduce_fusion.4
  68.8 0.1 eq.197
  69.1 0.2 reduce_window_sum.23
  69.3 0.2 select_reduce_fusion.2
  69.5 0.1 reduce_sum.81
  69.7 0.1 reduce_sum.83
  69.8 0.1 reduce_sum.87
  70.0 0.2 slice_reduce_fusion.1
  70.3 3.8 %collective-permute-done.4 = bf16[64,2048]{1,0:T(8,128)(2,1)S(1)} collective-permute-done((bf16[64,2048]{1,0:T(8,128)(2,1)S(1)}, bf16[64,2048]{1,0:T(8,128)(2,1)S(1)}, u32[]{:S(2)}, u32[]{:S(2)}) %collective-permute-start.4) | collective-permute-done | bytes 262176 | tf_op jit(solution)/shard_map/ppermute | solution.py:19
  74.0 0.2 multiply_reduce_fusion
  74.4 0.2 fusion.4
  74.6 1.2 convolution_convert_fusion
  75.7 46.6 %all_to_all.10.rows_in = bf16[32,24,2048]{2,1,0:T(8,128)(2,1)S(1)} all-to-all(bf16[32,24,2048]{2,1,0:T(8,128)(2,1)S(1)} %bitcast.47), channel_id=1, replica_groups=mesh['section'=16,'side'=2,'plane'=32] {'section','side'}, dimensions={0} | all-to-all | bytes 6291456 | tf_op jit(solution)/shard_map/all_to_all | solution.py:319
  122.3 87.1 %all-gather.3.cloned.1.call-done = bf16[36864,128]{1,0:T(8,128)(2,1)} async-done(((bf16[1152,128]{1,0:T(8,128)(2,1)}), bf16[36864,128]{1,0:T(8,128)(2,1)}) %all-gather.3.cloned.1.call-update) | async-done | bytes 9437200 | tf_op jit(solution)/shard_map/all_gather | solution.py:280
  209.4 10.9 %shard_map.83 = bf16[32,24,2048]{2,1,0:T(8,128)(2,1)} custom-call(s32[1]{0:T(128)} %bitcast.19.place, bf16[32,24,2048]{2,1,0:T(8,128)(2,1)S(1)} %all_to_all.10.rows_in, bf16[32,9,2,64,128]{4,3,2,1,0:T(8,128)(2,1)} %bitcast.65), custom_call_target="tpu_custom_call" | custom-call | flops 7247757312 | bytes 15728640 | tf_op jit(solution)/shard_map/pallas_call | solution.py:134
  220.3 7.7 %all-to-all-start.1 = ((bf16[32,24,2048]{2,1,0:T(8,128)(2,1)}), bf16[32,24,2048]{2,1,0:T(8,128)(2,1)S(1)}, u32[]{:S(2)}, u32[]{:S(2)}) async-start(bf16[32,24,2048]{2,1,0:T(8,128)(2,1)} %shard_map.83), calls=%async_computation.1 | async-start | bytes 6291456 | tf_op jit(solution)/shard_map/all_to_all | solution.py:319
  228.3 42.6 %all-to-all-done.1 = bf16[32,24,2048]{2,1,0:T(8,128)(2,1)S(1)} async-done(((bf16[32,24,2048]{2,1,0:T(8,128)(2,1)}), bf16[32,24,2048]{2,1,0:T(8,128)(2,1)S(1)}, u32[]{:S(2)}, u32[]{:S(2)}) %all-to-all-start.1) | async-done | bytes 3145760 | tf_op jit(solution)/shard_map/all_to_all | solution.py:319
  270.8 2.9 %fusion.2 = bf16[2,1,64,2048]{3,2,1,0:T(8,128)(2,1)} fusion(bf16[768,2048,1]{1,0,2:T(8,128)(2,1)S(1)} %bitcast.48, pred[2]{0:T(512)(128)(4,1)S(1)} %pad_add_fusion, s32[2,64]{1,0:T(2,128)S(1)} %eq.219, s32[2,64]{1,0:T(2,128)S(1)} %eq.215, f32[2,64]{1,0:T(2,128)S(1)} %bitcast.64, s32[2,64]{1,0:T(2,128)S(1)} %eq.210, f32[2,64]{1,0:T(2,128)S(1)} %bitcast.63, ...), kind=kOutput, calls=%fused_computation.4 | convolution fusion | flops 1210056704 | bytes 4197378 | tf_op jit(solution)/shard_map/dot_general | solution.py:325
  (43 shorter events, 1.5 us)
Async XLA Ops:
  6.5 51.3 %copy-start.3 = (s32[64]{0:T(128)S(1)}, s32[64]{0:T(128)}, u32[]{:S(2)}) copy-start(s32[64]{0:T(128)} %placement.1) | copy-start | bytes 772
  6.5 45.7 %copy-start.4 = (s32[2,1,64,2]{2,3,1,0:T(2,128)S(1)}, s32[2,1,64,2]{2,3,1,0:T(2,128)}, u32[]{:S(2)}) copy-start(s32[2,1,64,2]{2,3,1,0:T(2,128)} %param.10) | copy-start | bytes 3076
  6.5 45.7 %copy-start.5 = (f32[2,1,64,2]{2,3,1,0:T(2,128)S(1)}, f32[2,1,64,2]{2,3,1,0:T(2,128)}, u32[]{:S(2)}) copy-start(f32[2,1,64,2]{2,3,1,0:T(2,128)} %param.11) | copy-start | bytes 3076
  6.5 57.1 %copy-start.1 = (bf16[2,1,64,2048]{3,2,1,0:T(8,128)(2,1)S(1)}, bf16[2,1,64,2048]{3,2,1,0:T(8,128)(2,1)}, u32[]{:S(2)}) copy-start(bf16[2,1,64,2048]{3,2,1,0:T(8,128)(2,1)} %param.8) | copy-start | bytes 1572868
  6.5 202.9 %all-gather.3.cloned.1.call-start = ((), (), s32[]{:S(2)}) async-start(), calls=%async_computation.2 | async-start | bytes 9732096 | tf_op jit(solution)/shard_map/all_gather | solution.py:280
  9.4 35.1 %collective-permute-start = (bf16[576,128]{1,0:T(8,128)(2,1)}, bf16[576,128]{1,0:T(8,128)(2,1)S(1)}, u32[]{:S(2)}, u32[]{:S(2)}) collective-permute-start(bf16[576,128]{1,0:T(8,128)(2,1)} %get-tuple-element.11), channel_id=1, source_target_pairs={{0,24},{1,25},{2,26},{3,27},{4,28},{5,29},{6,30},{7,31},{8,0},{9,1... | collective-permute-start | bytes 442376 | tf_op jit(solution)/shard_map/ppermute | solution.py:257
  32.0 18.4 %collective-permute-start.2 = (bf16[576,128]{1,0:T(8,128)(2,1)}, bf16[576,128]{1,0:T(8,128)(2,1)S(1)}, u32[]{:S(2)}, u32[]{:S(2)}) collective-permute-start(bf16[576,128]{1,0:T(8,128)(2,1)} %get-tuple-element.12), channel_id=1, source_target_pairs={{0,7},{1,8},{2,9},{3,10},{4,11},{5,12},{6,13},{7,14},{8,15},{9,16}... | collective-permute-start | bytes 442376 | tf_op jit(solution)/shard_map/ppermute | solution.py:257
  44.5 7.8 %collective-permute-start.1 = (bf16[576,128]{1,0:T(8,128)(2,1)S(1)}, bf16[576,128]{1,0:T(8,128)(2,1)S(1)}, u32[]{:S(2)}, u32[]{:S(2)}) collective-permute-start(bf16[576,128]{1,0:T(8,128)(2,1)S(1)} %collective-permute-done), channel_id=1, source_target_pairs={{0,512},{1,577},{2,642},{3,707},{4,772},{5,837},{6,902},{7,967},{8... | collective-permute-start | bytes 442376 | tf_op jit(solution)/shard_map/ppermute | solution.py:264
  50.3 6.5 %collective-permute-start.3 = (bf16[576,128]{1,0:T(8,128)(2,1)S(1)}, bf16[576,128]{1,0:T(8,128)(2,1)S(1)}, u32[]{:S(2)}, u32[]{:S(2)}) collective-permute-start(bf16[576,128]{1,0:T(8,128)(2,1)S(1)} %collective-permute-done.2), channel_id=1, source_target_pairs={{0,576},{1,641},{2,706},{3,771},{4,836},{5,901},{6,966},{7,7},{8,7... | collective-permute-start | bytes 442376 | tf_op jit(solution)/shard_map/ppermute | solution.py:264
  56.8 17.6 %copy-start.2 = (f32[2048]{0:T(1024)S(1)}, f32[2048]{0:T(1024)}, u32[]{:S(2)}) copy-start(f32[2048]{0:T(1024)} %param.9) | copy-start | bytes 24580
  58.0 10.6 %collective-permute-start.6 = (f32[64,4]{0,1:T(4,128)S(1)}, f32[64,4]{0,1:T(4,128)S(1)}, u32[]{:S(2)}, u32[]{:S(2)}) collective-permute-start(f32[64,4]{0,1:T(4,128)S(1)} %get-tuple-element.33), channel_id=1, source_target_pairs={{0,64},{64,128},{128,192},{192,256},{256,320},{320,384},{384,448},... | collective-permute-start | bytes 3080 | tf_op jit(solution)/shard_map/ppermute | solution.py:19
  59.9 8.6 %collective-permute-start.7 = (f32[64,4]{0,1:T(4,128)S(1)}, f32[64,4]{0,1:T(4,128)S(1)}, u32[]{:S(2)}, u32[]{:S(2)}) collective-permute-start(f32[64,4]{0,1:T(4,128)S(1)} %get-tuple-element.32), channel_id=1, source_target_pairs={{64,0},{128,64},{192,128},{256,192},{320,256},{384,320},{448,384},... | collective-permute-start | bytes 3080 | tf_op jit(solution)/shard_map/ppermute | solution.py:19
  63.7 6.6 %collective-permute-start.5 = (bf16[64,2048]{1,0:T(8,128)(2,1)S(1)}, bf16[64,2048]{1,0:T(8,128)(2,1)S(1)}, u32[]{:S(2)}, u32[]{:S(2)}) collective-permute-start(bf16[64,2048]{1,0:T(8,128)(2,1)S(1)} %get-tuple-element.27), channel_id=1, source_target_pairs={{64,0},{128,64},{192,128},{256,192},{320,256},{384,320},{448,384},... | collective-permute-start | bytes 786440 | tf_op jit(solution)/shard_map/ppermute | solution.py:19
  66.3 7.7 %collective-permute-start.4 = (bf16[64,2048]{1,0:T(8,128)(2,1)S(1)}, bf16[64,2048]{1,0:T(8,128)(2,1)S(1)}, u32[]{:S(2)}, u32[]{:S(2)}) collective-permute-start(bf16[64,2048]{1,0:T(8,128)(2,1)S(1)} %get-tuple-element.26), channel_id=1, source_target_pairs={{0,64},{64,128},{128,192},{192,256},{256,320},{320,384},{384,448},... | collective-permute-start | bytes 786440 | tf_op jit(solution)/shard_map/ppermute | solution.py:19
  74.0 1.7 copy-start
  220.3 50.6 %all-to-all-start.1 = ((bf16[32,24,2048]{2,1,0:T(8,128)(2,1)}), bf16[32,24,2048]{2,1,0:T(8,128)(2,1)S(1)}, u32[]{:S(2)}, u32[]{:S(2)}) async-start(bf16[32,24,2048]{2,1,0:T(8,128)(2,1)} %shard_map.83), calls=%async_computation.1 | async-start | bytes 6291456 | tf_op jit(solution)/shard_map/all_to_all | solution.py:319
Sparse Core Ops, SparseCore 0:
  57.7 151.6 all-gather.2
